TPU v7x, 32 devices: a whole 2x2x4 slice. The times are simulated.
32 devices in a mesh: section: 4 (over y, x), rows: 8 (over z, core).
Axes of the slice: x: 2, y: 2, z: 4, core: 2. Of those that a mesh axis runs over, the one named last changes fastest.
Arguments:
- tokens: bfloat16 [8, 2048, 768], P(None, 'rows'), may hold values from -6 to 6
- cotangent: bfloat16 [8, 2048, 768], P(None, 'rows'), may hold values from -6 to 6
- segment_ids: int32 [8, 2048], replicated, may hold values from 0 to 15, never falling along the last dimension, each value on 1 to 256 neighbouring positions
- slabs: bfloat16 [4, 768, 3072], P('section'), as said below
- ffn_down: bfloat16 [2, 3072, 768], replicated, may hold values from -0.109375 to 0.109375
- ad_down: float32 [4, 768, 64], P('section'), may hold values from -0.21875 to 0.21875
- ad_down_bias: float32 [4, 64], P('section'), may hold values from -3 to 3
- ad_up: float32 [4, 64, 768], P('section'), may hold values from -0.75 to 0.75
- ad_up_bias: float32 [4, 768], P('section'), may hold values from -2 to 2
- ln_gain: float32 [4, 768], P('section'), may hold values from 0.5 to 1.5
- ln_bias: float32 [4, 768], P('section'), may hold values from -2 to 2
Outputs:
- block_outputs: bfloat16 [4, 8, 2048, 768], P('section', None, 'rows')
- input_grads: bfloat16 [4, 8, 2048, 768], P('section', None, 'rows')
- grad_ad_down: float32 [4, 768, 64], P('section')
- grad_ad_down_bias: float32 [4, 64], P('section')
- grad_ad_up: float32 [4, 64, 768], P('section')
- grad_ad_up_bias: float32 [4, 768], P('section')
- grad_ln_gain: float32 [4, 768], P('section')
- grad_ln_bias: float32 [4, 768], P('section')
Inputs may be any that keep to these rules, and one draw needn't show every extreme that they name: `segment_ids`: along each micro-batch the ids never fall; every id of 0 to 15 appears, each segment covers 1 to 256 rows and one covers exactly 256. For even b, columns 2304 to 3072 of slabs[b] are an output projection of larger entries than the other columns.
All inputs are finite; a program needn't handle non-finite values.
Results may differ from a plain program's by a relative error of at most 0.02.
Values may be sent and summed in bfloat16 or wider, within the bound.
No kernel may reach another device: no remote copies, remote signals or barrier semaphores. Data moves between devices by JAX's collectives and lax.ppermute only.
A program may use at most 192 MiB of HBM per device.

v0:
```python
import functools

import jax
import jax.numpy as jnp
from jax import lax
from jax.experimental import pallas as pl
from jax.experimental.pallas import tpu as pltpu
from jax.sharding import PartitionSpec as P

HEADS = 12
GROUP = 2
EXTRA = 32
BF = jnp.bfloat16
F32 = jnp.float32
VMEM = pl.BlockSpec(memory_space=pltpu.VMEM)
ANY = pl.BlockSpec(memory_space=pl.ANY)
SMEM = pl.BlockSpec(memory_space=pltpu.SMEM)
LIMIT = 56 * 1024 * 1024


def dot(left, right):
    return jnp.dot(left, right, preferred_element_type=F32)


def dot_t(left, right):
    return lax.dot_general(left, right, (((1,), (1,)), ((), ())), preferred_element_type=F32)


def gelu_pair(x):
    t = 1.0 / (1.0 + 0.23164188 * jnp.abs(x))
    poly = t * (0.127414796 + t * (-0.142248368 + t * (0.710706871 + t * (
        -0.726576014 + t * 0.530702715))))
    bell = jnp.exp(-0.5 * (x * x))
    tail = poly * bell
    phi = jnp.where(x < 0, tail, 1.0 - tail)
    return x * phi, phi + x * (0.3989422804014327 * bell)


class Weights:
    def __init__(self, src, own_slab, own_pack, bufs, slab_v, pack_v, sem):
        self.args = (src, own_slab, own_pack, bufs, slab_v, pack_v, sem)

    def start(self):
        src, own_slab, own_pack, bufs, slab_v, pack_v, sem = self.args
        half = own_slab.shape[0] // GROUP
        for h in range(GROUP):
            rows = pl.ds(h * half, half)

            @pl.when(src[h] == 0)
            def _():
                pltpu.make_async_copy(own_pack.at[h], pack_v.at[h], sem.at[h]).start()
                pltpu.make_async_copy(own_slab.at[rows], slab_v.at[rows], sem.at[2 + h]).start()

            for i, buf in enumerate(bufs):
                @pl.when(src[h] == i + 1)
                def _():
                    pltpu.make_async_copy(buf.at[pl.ds(half, EXTRA)], pack_v.at[h], sem.at[h]).start()
                    pltpu.make_async_copy(buf.at[pl.ds(0, half)], slab_v.at[rows], sem.at[2 + h]).start()

    def wait_slab(self):
        src, own_slab, own_pack, bufs, slab_v, pack_v, sem = self.args
        half = own_slab.shape[0] // GROUP
        for h in range(GROUP):
            rows = pl.ds(h * half, half)
            pltpu.make_async_copy(own_slab.at[rows], slab_v.at[rows], sem.at[2 + h]).wait()

    def wait_pack(self):
        src, own_slab, own_pack, bufs, slab_v, pack_v, sem = self.args
        for h in range(GROUP):
            pltpu.make_async_copy(own_pack.at[h], pack_v.at[h], sem.at[h]).wait()

    def adapters(self, width, adapt):
        pack_v = self.args[5]
        rows = [pack_v[0, :, i * width : (i + 1) * width] for i in range(4)]
        zeros = jnp.zeros((128 - adapt, width), BF)
        per = adapt // EXTRA
        down_t = jnp.concatenate(rows[:per] + [zeros], axis=0)
        up = jnp.concatenate(rows[per : 2 * per] + [zeros], axis=0)
        return down_t, up

    def small(self, i, width):
        pack_v = self.args[5]
        low = 2 * i
        return (pack_v[1, low : low + 1, :width].astype(F32)
                + pack_v[1, low + 1 : low + 2, :width].astype(F32))


def post_forward(wts, x_ref, b_ref, y_ref, saved, adapt):
    low_ref, ut_ref, slope_ref, zhat_ref, rstd_ref = saved
    rows, width = x_ref.shape
    wts.wait_pack()
    down_t, up = wts.adapters(width, adapt)
    down_bias, up_bias, gain, bias = [wts.small(i, width) for i in range(4)]
    step = 128

    def body(i, carry):
        at = pl.ds(pl.multiple_of(i * step, step), step)
        branch = b_ref[at, :]
        low = branch.astype(BF)
        low_ref[at, :] = low
        pre = dot_t(low, down_t) + down_bias[:, :128]
        inner, slope = gelu_pair(pre)
        slope_ref[at, :] = slope
        ut_ref[:, at] = inner.T.astype(BF)
        mixed = x_ref[at, :].astype(F32) + branch + dot(inner.astype(BF), up) + up_bias
        center = mixed - jnp.mean(mixed, axis=-1, keepdims=True)
        rstd = lax.rsqrt(jnp.mean(center * center, axis=-1, keepdims=True) + 1e-05)
        zhat = center * rstd
        y_ref[at, :] = (zhat * gain + bias).astype(BF)
        zhat_ref[at, :] = zhat.astype(BF)
        rstd_ref[at, :] = jnp.broadcast_to(rstd, (step, 128))
        return carry

    lax.fori_loop(0, rows // step, body, 0)


def post_backward(wts, dy_ref, saved, dz_ref, db_ref, grads_ref, dpt_ref, adapt):
    low_ref, ut_ref, slope_ref, zhat_ref, rstd_ref = saved
    rows, width = dy_ref.shape
    wts.wait_pack()
    down_t, up = wts.adapters(width, adapt)
    gain = wts.small(2, width)
    step = 128

    def fold(v):
        return jnp.sum(v.reshape(v.shape[0] // 8, 8, v.shape[1]), axis=0)

    def body(i, carry):
        s_bias, s_gain, s_upb, s_downb = carry
        at = pl.ds(pl.multiple_of(i * step, step), step)
        d_out = dy_ref[at, :].astype(F32)
        zhat = zhat_ref[at, :].astype(F32)
        s_bias = s_bias + fold(d_out)
        s_gain = s_gain + fold(d_out * zhat)
        dz = d_out * gain
        dz = rstd_ref[at, :1] * (dz - jnp.mean(dz, axis=-1, keepdims=True)
                                 - zhat * jnp.mean(dz * zhat, axis=-1, keepdims=True))
        s_upb = s_upb + fold(dz)
        low = dz.astype(BF)
        db_ref[at, :] = low
        d_pre = dot_t(low, up) * slope_ref[at, :]
        s_downb = s_downb + fold(d_pre)
        dpt_ref[:, at] = d_pre.T.astype(BF)
        dz_ref[at, :] = dz
        return s_bias, s_gain, s_upb, s_downb

    zero = jnp.zeros((8, width), F32)
    s_bias, s_gain, s_upb, s_downb = lax.fori_loop(
        0, rows // step, body, (zero, zero, zero, jnp.zeros((8, 128), F32)))
    g_down = dot(dpt_ref[...], low_ref[...])
    g_up = dot(ut_ref[...], db_ref[...])
    grads_ref[0:adapt, :] = g_down[:adapt].astype(BF)
    grads_ref[adapt : 2 * adapt, :] = g_up[:adapt].astype(BF)
    tail = jnp.concatenate(
        [jnp.sum(v, axis=0, keepdims=True) for v in (s_upb, s_gain, s_bias)]
        + [jnp.concatenate([jnp.sum(s_downb, axis=0, keepdims=True),
                            jnp.zeros((1, width - 128), F32)], axis=1),
           jnp.zeros((12, width), F32)], axis=0)
    grads_ref[2 * adapt :, :] = tail.astype(BF)

    def body2(i, carry):
        at = pl.ds(pl.multiple_of(i * step, step), step)
        d_pre = dpt_ref[:, at].astype(F32).T.astype(BF)
        db_ref[at, :] = (dz_ref[at, :] + dot(d_pre, down_t)).astype(BF)
        return carry

    lax.fori_loop(0, rows // step, body2, 0)


def saved_shapes(rows, width):
    return [
        jax.ShapeDtypeStruct((rows, width), BF),
        jax.ShapeDtypeStruct((128, rows), BF),
        jax.ShapeDtypeStruct((rows, 128), F32),
        jax.ShapeDtypeStruct((rows, width), BF),
        jax.ShapeDtypeStruct((rows, 128), F32),
    ]


def weight_scratch(slab):
    return [
        pltpu.VMEM(slab.shape, BF),
        pltpu.VMEM((GROUP, EXTRA, slab.shape[1]), BF),
        pltpu.SemaphoreType.DMA((2 * GROUP,)),
    ]


def call(body, outs, out_specs, scratch, n_smem, in_specs, flops, nbytes, trans, name):
    return pl.pallas_call(
        body,
        out_shape=outs,
        in_specs=[SMEM] * n_smem + in_specs,
        out_specs=out_specs,
        scratch_shapes=scratch,
        name=name,
        cost_estimate=pl.CostEstimate(flops=flops, bytes_accessed=nbytes, transcendentals=trans),
        compiler_params=pltpu.CompilerParams(vmem_limit_bytes=LIMIT),
    )


def ffn_forward(x, src, weights, down, adapt):
    own_slab, own_pack, bufs = weights
    rows, width = x.shape
    ff = own_slab.shape[1]
    chunk = 512
    n_buf = len(bufs)

    def body(src_ref, x_ref, own_ref, pack_ref, *rest):
        bufs_ref, rest = rest[:n_buf], rest[n_buf:]
        down_ref, y_ref, act_ref, *rest = rest
        saved, (slab_v, pack_v, sem, down_v, down_sem, acc) = rest[:5], rest[5:]
        wts = Weights(src_ref, own_ref, pack_ref, bufs_ref, slab_v, pack_v, sem)
        wts.start()
        copy = pltpu.make_async_copy(down_ref, down_v, down_sem)
        copy.start()
        wts.wait_slab()
        copy.wait()

        def step(j, carry):
            cols = pl.ds(pl.multiple_of(j * chunk, chunk), chunk)
            act, slope = gelu_pair(dot(x_ref[...], slab_v[:, cols]))
            act_ref[:, cols] = slope.astype(BF)
            part = dot(act.astype(BF), down_v[cols, :])

            @pl.when(j == 0)
            def _():
                acc[...] = part

            @pl.when(j > 0)
            def _():
                acc[...] += part
            return carry

        lax.fori_loop(0, ff // chunk, step, 0)
        post_forward(wts, x_ref, acc, y_ref, saved, adapt)

    outs = [jax.ShapeDtypeStruct((rows, width), BF), jax.ShapeDtypeStruct((rows, ff), BF)]
    outs += saved_shapes(rows, width)
    scratch = weight_scratch(own_slab) + [
        pltpu.VMEM((ff, width), BF), pltpu.SemaphoreType.DMA, pltpu.VMEM((rows, width), F32)]
    res = call(body, outs, [VMEM] * len(outs), scratch, 1,
               [VMEM, ANY, ANY] + [ANY] * n_buf + [ANY],
               4 * rows * width * ff, 4 * width * ff + 16 * rows * width, rows * ff, "ffn_forward")(
        src, x, own_slab, own_pack, *bufs, down)
    return res[0], tuple(res[1:])


def ffn_backward(dy, saved, src, weights, down, adapt):
    own_slab, own_pack, bufs = weights
    rows, width = dy.shape
    ff = own_slab.shape[1]
    chunk = 512
    n_buf = len(bufs)
    act, saved = saved[0], saved[1:]

    def body(src_ref, dy_ref, *rest):
        saved_ref, rest = rest[:5], rest[5:]
        act_ref, own_ref, pack_ref, *rest = rest
        bufs_ref, rest = rest[:n_buf], rest[n_buf:]
        (down_ref, dx_ref, grads_ref, slab_v, pack_v, sem, down_v, act_v, big_sem, acc, db,
         dpt) = rest
        wts = Weights(src_ref, own_ref, pack_ref, bufs_ref, slab_v, pack_v, sem)
        wts.start()
        copy_down = pltpu.make_async_copy(down_ref, down_v, big_sem.at[0])
        copy_down.start()
        copy_act = pltpu.make_async_copy(act_ref, act_v, big_sem.at[1])
        copy_act.start()
        post_backward(wts, dy_ref, saved_ref, acc, db, grads_ref, dpt, adapt)
        wts.wait_slab()
        copy_down.wait()
        copy_act.wait()

        def step(j, carry):
            cols = pl.ds(pl.multiple_of(j * chunk, chunk), chunk)
            dg = dot_t(db[...], down_v[cols, :])
            df = (dg * act_v[:, cols].astype(F32)).astype(BF)
            acc[...] += dot_t(df, slab_v[:, cols])
            return carry

        lax.fori_loop(0, ff // chunk, step, 0)
        dx_ref[...] = acc[...].astype(BF)

    outs = [jax.ShapeDtypeStruct((rows, width), BF),
            jax.ShapeDtypeStruct((2 * adapt + 16, width), BF)]
    scratch = weight_scratch(own_slab) + [
        pltpu.VMEM((ff, width), BF), pltpu.VMEM((rows, ff), BF), pltpu.SemaphoreType.DMA((2,)),
        pltpu.VMEM((rows, width), F32), pltpu.VMEM((rows, width), BF),
        pltpu.VMEM((128, rows), BF)]
    return call(body, outs, [VMEM] * 2, scratch, 1,
                [VMEM] * 6 + [ANY] * (3 + n_buf) + [ANY],
                4 * rows * width * ff, 4 * width * ff + 16 * rows * width, 0, "ffn_backward")(
        src, dy, *saved, act, own_slab, own_pack, *bufs, down)


def attn_forward(x, seg, src, weights, adapt):
    own_slab, own_pack, bufs = weights
    rows, width = x.shape
    n_buf = len(bufs)
    head = width // HEADS
    pairs = HEADS // 2
    cols_step = 256

    def body(src_ref, x_ref, segc_ref, segr_ref, own_ref, pack_ref, *rest):
        bufs_ref, rest = rest[:n_buf], rest[n_buf:]
        y_ref, qkv_ref, p_ref, c_ref, *rest = rest
        saved, (slab_v, pack_v, sem, acc, bias_v, p_v, p_sem) = rest[:5], rest[5:]
        wts = Weights(src_ref, own_ref, pack_ref, bufs_ref, slab_v, pack_v, sem)
        wts.start()
        bias_v[...] = jnp.where(segc_ref[...] == segr_ref[...], 0.0, -1e30)
        wts.wait_slab()

        def project(j, carry):
            cols = pl.ds(pl.multiple_of(j * cols_step, cols_step), cols_step)
            scale = jnp.where(j < width // cols_step, head ** -0.5, 1.0)
            qkv_ref[:, cols] = (dot(x_ref[...], slab_v[:, cols]) * scale).astype(BF)
            return carry

        lax.fori_loop(0, 3 * width // cols_step, project, 0)
        lower = lax.broadcasted_iota(jnp.int32, (rows, 2 * head), 1) < head

        def attend(i, carry):
            def cols_of(part):
                return pl.ds(pl.multiple_of(part * width + i * 2 * head, 2 * head), 2 * head)

            q, k, v = qkv_ref[:, cols_of(0)], qkv_ref[:, cols_of(1)], qkv_ref[:, cols_of(2)]
            parts = []
            for h in range(2):
                q_h = jnp.where(lower == (h == 0), q, jnp.zeros_like(q))
                s = dot_t(q_h, k) + bias_v[...]
                e = jnp.exp(s - jnp.max(s, axis=-1, keepdims=True))
                p = (e * (1.0 / jnp.sum(e, axis=-1, keepdims=True))).astype(BF)
                p_v[2 * i + h] = p
                pltpu.make_async_copy(p_v.at[2 * i + h], p_ref.at[2 * i + h], p_sem).start()
                parts.append(dot(p, v))
            c_ref[:, pl.ds(pl.multiple_of(i * 2 * head, 2 * head), 2 * head)] = jnp.where(
                lower, parts[0], parts[1]).astype(BF)
            return carry

        lax.fori_loop(0, pairs, attend, 0)

        def output(j, carry):
            cols = pl.ds(pl.multiple_of(j * cols_step, cols_step), cols_step)
            acc[:, cols] = dot(c_ref[...], slab_v[:, pl.ds(
                pl.multiple_of(3 * width + j * cols_step, cols_step), cols_step)])
            return carry

        lax.fori_loop(0, width // cols_step, output, 0)
        post_forward(wts, x_ref, acc, y_ref, saved, adapt)
        pltpu.make_async_copy(p_v, p_ref, p_sem).wait()

    outs = [jax.ShapeDtypeStruct((rows, width), BF), jax.ShapeDtypeStruct((rows, 3 * width), BF),
            jax.ShapeDtypeStruct((HEADS, rows, rows), BF), jax.ShapeDtypeStruct((rows, width), BF)]
    specs = [VMEM, VMEM, ANY, VMEM] + [VMEM] * 5
    outs += saved_shapes(rows, width)
    scratch = weight_scratch(own_slab) + [
        pltpu.VMEM((rows, width), F32), pltpu.VMEM((rows, rows), F32),
        pltpu.VMEM((HEADS, rows, rows), BF), pltpu.SemaphoreType.DMA]
    res = call(body, outs, specs, scratch, 1, [VMEM] * 3 + [ANY] * (2 + n_buf),
               8 * rows * width * width + 4 * rows * rows * width,
               8 * width * width + 2 * HEADS * rows * rows + 16 * rows * width,
               HEADS * rows * rows, "attn_forward")(
        src, x, seg[:, None], seg[None, :], own_slab, own_pack, *bufs)
    return res[0], tuple(res[1:])


def attn_backward(dy, saved, src, weights, adapt):
    own_slab, own_pack, bufs = weights
    rows, width = dy.shape
    n_buf = len(bufs)
    head = width // HEADS
    pairs = HEADS // 2
    cols_step = 256
    qkv, probs, ctx = saved[:3]
    saved = saved[3:]

    def body(src_ref, dy_ref, *rest):
        saved_ref, rest = rest[:5], rest[5:]
        qkv_ref, c_ref, p_ref, own_ref, pack_ref, *rest = rest
        bufs_ref, rest = rest[:n_buf], rest[n_buf:]
        (dx_ref, grads_ref, slab_v, pack_v, sem, p_v, p_sem, dz, db, dpt, dc_v, dqkv) = rest
        wts = Weights(src_ref, own_ref, pack_ref, bufs_ref, slab_v, pack_v, sem)
        wts.start()
        copy_p = pltpu.make_async_copy(p_ref, p_v, p_sem)
        copy_p.start()
        post_backward(wts, dy_ref, saved_ref, dz, db, grads_ref, dpt, adapt)
        wts.wait_slab()

        def context(j, carry):
            cols = pl.ds(pl.multiple_of(j * cols_step, cols_step), cols_step)
            dc_v[:, cols] = dot_t(db[...], slab_v[cols, 3 * width :]).astype(BF)
            return carry

        lax.fori_loop(0, width // cols_step, context, 0)
        copy_p.wait()
        lower = lax.broadcasted_iota(jnp.int32, (rows, 2 * head), 1) < head

        def attend(i, carry):
            def cols_of(part):
                return pl.ds(pl.multiple_of(part * width + i * 2 * head, 2 * head), 2 * head)

            q, k, v = qkv_ref[:, cols_of(0)], qkv_ref[:, cols_of(1)], qkv_ref[:, cols_of(2)]
            dc = dc_v[:, cols_of(0)]
            dc_wide = dc.astype(F32)
            prod = dc_wide * c_ref[:, cols_of(0)].astype(F32)
            q_t = q.astype(F32).T.astype(BF)
            dc_t = dc_wide.T.astype(BF)
            dq, dk, dv = [], [], []
            for h in range(2):
                mine = lower == (h == 0)
                p = p_v[2 * i + h]
                delta = jnp.sum(jnp.where(mine, prod, 0.0), axis=-1, keepdims=True)
                dp = dot_t(jnp.where(mine, dc, jnp.zeros_like(dc)), v)
                ds = (p.astype(F32) * (dp - delta)).astype(BF)
                dq.append(dot(ds, k))
                dk.append(dot(q_t[h * head : (h + 1) * head], ds))
                dv.append(dot(dc_t[h * head : (h + 1) * head], p))
            dqkv[:, cols_of(0)] = (jnp.where(lower, dq[0], dq[1]) * head ** -0.5).astype(BF)
            dqkv[:, cols_of(1)] = jnp.concatenate(dk, axis=0).T.astype(BF)
            dqkv[:, cols_of(2)] = jnp.concatenate(dv, axis=0).T.astype(BF)
            return carry

        lax.fori_loop(0, pairs, attend, 0)

        def output(j, carry):
            cols = pl.ds(pl.multiple_of(j * cols_step, cols_step), cols_step)
            dx_ref[:, cols] = (dz[:, cols] + dot_t(dqkv[...], slab_v[cols, : 3 * width])).astype(BF)
            return carry

        lax.fori_loop(0, width // cols_step, output, 0)

    outs = [jax.ShapeDtypeStruct((rows, width), BF),
            jax.ShapeDtypeStruct((2 * adapt + 16, width), BF)]
    scratch = weight_scratch(own_slab) + [
        pltpu.VMEM((HEADS, rows, rows), BF), pltpu.SemaphoreType.DMA,
        pltpu.VMEM((rows, width), F32), pltpu.VMEM((rows, width), BF),
        pltpu.VMEM((128, rows), BF), pltpu.VMEM((rows, width), BF),
        pltpu.VMEM((rows, 3 * width), BF)]
    return call(body, outs, [VMEM] * 2, scratch, 1,
                [VMEM] * 8 + [ANY] * (3 + n_buf),
                8 * rows * width * width + 8 * rows * rows * width,
                8 * width * width + 2 * HEADS * rows * rows + 16 * rows * width, 0,
                "attn_backward")(
        src, dy, *saved, qkv, ctx, probs, own_slab, own_pack, *bufs)


def split_rows(v):
    high = v.astype(BF)
    return high, (v - high.astype(F32)).astype(BF)


def pack_adapters(ad_down, down_bias, ad_up, up_bias, gain, bias):
    width, adapt = ad_down.shape
    mats = jnp.concatenate([ad_down.T, ad_up], axis=0).astype(BF)
    mats = jnp.concatenate([mats[i : i + EXTRA] for i in range(0, 2 * adapt, EXTRA)], axis=1)
    rows = []
    for v in (jnp.pad(down_bias, (0, width - adapt)), up_bias, gain, bias):
        rows += list(split_rows(v))
    rows = jnp.pad(jnp.stack(rows), ((0, EXTRA - len(rows)), (0, mats.shape[1] - width)))
    return jnp.stack([mats, rows])


def per_device(tokens, cotangent, segment_ids, slabs, ffn_down,
               ad_down, ad_down_bias, ad_up, ad_up_bias, ln_gain, ln_bias):
    n_section = lax.axis_size("section")
    n_rows = lax.axis_size("rows")
    s = lax.axis_index("section")
    r = lax.axis_index("rows")
    core = r % GROUP
    n_micro, rows_dev, width = tokens.shape
    adapt = ad_down.shape[2]

    def sect(x, apart):
        return lax.ppermute(x, "section", [(i, i ^ apart) for i in range(n_section)])

    def peer(x, apart=1):
        return lax.ppermute(x, "rows", [(i, i ^ apart) for i in range(n_rows)])

    own_micro = s * GROUP + core
    peer_micro = s * GROUP + 1 - core

    def gather_item(x):
        mine = lax.dynamic_index_in_dim(x, own_micro, 0, keepdims=False)
        given = lax.dynamic_index_in_dim(x, peer_micro, 0, keepdims=False)
        return jnp.concatenate([mine, peer(given)], axis=0)

    hidden = gather_item(tokens)
    cot = gather_item(cotangent)
    seg_a = lax.dynamic_slice(segment_ids, (own_micro, r * rows_dev), (1, rows_dev))[0]
    seg_b = lax.dynamic_slice(segment_ids, (own_micro, (r ^ 1) * rows_dev), (1, rows_dev))[0]
    seg = jnp.concatenate([seg_a, seg_b])

    slab = slabs[0]
    half = slab.shape[0] // GROUP
    own_pack = pack_adapters(ad_down[0], ad_down_bias[0], ad_up[0], ad_up_bias[0], ln_gain[0],
                             ln_bias[0])
    given = jnp.concatenate([
        lax.dynamic_slice_in_dim(slab, core * half, half, 0),
        lax.dynamic_index_in_dim(own_pack, core, 0, keepdims=False)], axis=0)
    mine = [sect(given, d) for d in range(1, n_section)]
    other = [peer(x) for x in mine]
    weights = (slab, own_pack, tuple(mine + other))

    def source(b):
        d = s ^ b
        at = [jnp.where(d == 0, 0, jnp.where(core == h, d, d + n_section - 1)) for h in range(GROUP)]
        return jnp.stack(at).astype(jnp.int32)

    src = [source(b) for b in range(n_section)]
    outs, saves = [], []
    for b in range(n_section):
        if b % 2 == 0:
            hidden, saved = attn_forward(hidden, seg, src[b], weights, adapt)
        else:
            hidden, saved = ffn_forward(hidden, src[b], weights, ffn_down[b // 2], adapt)
        outs.append(hidden)
        saves.append(saved)

    def pick(pieces, b):
        return lax.dynamic_index_in_dim(pieces, s ^ b, 0, keepdims=False)

    def distribute(pieces):
        all_b = jnp.stack(pieces)
        other = peer(all_b[:, rows_dev:])
        mine = all_b[:, :rows_dev]
        both = jnp.where(core == 0, jnp.stack([mine, other], axis=1), jnp.stack([other, mine], axis=1))
        got = [pick(both, 0)]
        got = [lax.dynamic_index_in_dim(both, s, 0, keepdims=False)]
        for d in range(1, n_section):
            got.append(sect(lax.dynamic_index_in_dim(both, s ^ d, 0, keepdims=False), d))
        got = jnp.stack(got)
        return jnp.concatenate([pick(got, q) for q in range(n_section)], axis=0)[None]

    block_outputs = distribute(outs)
    grad = cot
    grads, packs = [None] * n_section, [None] * n_section
    for b in reversed(range(n_section)):
        if b % 2 == 0:
            grad, packs[b] = attn_backward(grad, saves[b], src[b], weights, adapt)
        else:
            grad, packs[b] = ffn_backward(grad, saves[b], src[b], weights, ffn_down[b // 2], adapt)
        grads[b] = grad
    input_grads = distribute(grads)

    total = jnp.stack(packs)
    apart = n_section // 2
    while apart >= 1:
        high = (s // apart) % 2
        keep = lax.dynamic_slice_in_dim(total, high * apart, apart, 0)
        give = lax.dynamic_slice_in_dim(total, (1 - high) * apart, apart, 0)
        total = (keep.astype(F32) + sect(give, apart).astype(F32)).astype(BF)
        apart //= 2
    total = total[0]
    apart = 1
    while apart < n_rows:
        total = (total.astype(F32) + peer(total, apart).astype(F32)).astype(BF)
        apart *= 2
    total = total.astype(F32)
    return (block_outputs, input_grads, total[:adapt].T[None], total[2 * adapt + 3, :adapt][None],
            total[adapt : 2 * adapt][None], total[2 * adapt][None], total[2 * adapt + 1][None],
            total[2 * adapt + 2][None])


def solution(mesh):
    in_specs = (
        P(None, "rows", None), P(None, "rows", None), P(), P("section", None, None), P(),
        P("section", None, None), P("section", None), P("section", None, None),
        P("section", None), P("section", None), P("section", None),
    )
    out_specs = (
        P("section", None, "rows", None), P("section", None, "rows", None),
        P("section", None, None), P("section", None), P("section", None, None),
        P("section", None), P("section", None), P("section", None),
    )
    return jax.shard_map(
        per_device, mesh=mesh, in_specs=in_specs, out_specs=out_specs, check_vma=False
    )
```

profile of v0, /device:TPU:0, one launch (start us, length us, event | category | flops | bytes accessed | tf_op | source)
XLA Modules:
  0.0 415.4 jit_solution(18349143296204087960)
XLA Ops:
  0.6 0.7 pad_convert_fusion
  1.3 0.7 fusion.4
  2.0 0.8 subtract_convert_fusion.2
  2.8 0.8 subtract_convert_fusion
  3.6 0.9 convert_bitcast_fusion
  4.6 0.9 convert.10
  5.5 1.8 dynamic-slice_bitcast_fusion
  7.7 3.0 collective-permute-start.1
  10.7 1.5 collective-permute-start.2
  12.2 54.7 %collective-permute-done.1.rest_0_.rest_8_.rest_10_ = bf16[416,3072]{1,0:T(8,128)(2,1)S(1)} collective-permute-done((bf16[416,3072]{1,0:T(8,128)(2,1)S(1)}, bf16[416,3072]{1,0:T(8,128)(2,1)S(1)}, u32[]{:S(2)}, u32[]{:S(2)}) %collective-permute-start.1) | collective-permute-done | bytes 2555936 | tf_op jit(solution)/shard_map/ppermute | solution.py:473
  67.0 55.5 %collective-permute-done.2.rest_1_.rest_9_.rest_11_ = bf16[416,3072]{1,0:T(8,128)(2,1)} collective-permute-done((bf16[416,3072]{1,0:T(8,128)(2,1)S(1)}, bf16[416,3072]{1,0:T(8,128)(2,1)}, u32[]{:S(2)}, u32[]{:S(2)}) %collective-permute-start.2) | collective-permute-done | bytes 2555936 | tf_op jit(solution)/shard_map/ppermute | solution.py:473
  122.5 0.5 collective-permute-start.6
  123.0 2.0 dynamic-slice_bitcast_fusion.18
  125.0 1.9 dynamic-slice_bitcast_fusion.16
  127.0 0.5 collective-permute-start.11
  127.5 0.6 pad_add_fusion.1.src_ref
  128.1 0.6 pad_add_fusion.2
  128.7 0.8 fusion.7
  129.5 7.9 %slice_bitcast_fusion = (bf16[3072,768]{1,0:T(8,128)(2,1)}, bf16[3072,768]{1,0:T(8,128)(2,1)}) fusion(bf16[2,3072,768]{2,1,0:T(8,128)(2,1)} %param.15), kind=kLoop, calls=%fused_computation | loop fusion | bytes 18874368 | tf_op jit(solution)/shard_map/squeeze | solution.py:514
  137.4 0.6 pad_add_fusion.4.src_ref
  138.0 0.9 copy.19.segc_ref
  138.8 0.8 pad_maximum_fusion.8.pack_ref.rest_7_.rest_9_
  139.6 2.0 pad_maximum_fusion.6.x_ref
  141.6 1.9 pad_maximum_fusion.7.dy_ref
  143.6 21.8 %attn_forward.2 = (bf16[512,768]{1,0:T(8,128)(2,1)}, bf16[512,2304]{1,0:T(8,128)(2,1)}, bf16[12,512,512]{2,1,0:T(8,128)(2,1)}, bf16[512,768]{1,0:T(8,128)(2,1)},...) custom-call(s32[2]{0:T(128)} %pad_add_fusion.1.src_ref, ...), custom_call_target="tpu_custom_call" | custom-call | flops 3221225472 | bytes 17301504 | tf_op jit(solution)/shard_map/attn_forward/pallas_call | solution.py:358
  165.4 20.9 %ffn_forward.2 = (bf16[512,768]{1,0:T(8,128)(2,1)}, bf16[512,3072]{1,0:T(8,128)(2,1)}, bf16[512,768]{1,0:T(8,128)(2,1)}, bf16[128,512]{1,0:T(8,128)(2,1)}, f32[5...) custom-call(s32[2]{0:T(128)} %get-tuple-element.131.src_ref, ...), custom_call_target="tpu_custom_call" | custom-call | flops 4831838208 | bytes 15728640 | tf_op jit(solution)/shard_map/ffn_forward/pallas_call | solution.py:241
  186.4 21.8 %attn_forward.3 = (bf16[512,768]{1,0:T(8,128)(2,1)}, bf16[512,2304]{1,0:T(8,128)(2,1)}, bf16[12,512,512]{2,1,0:T(8,128)(2,1)}, bf16[512,768]{1,0:T(8,128)(2,1)},...) custom-call(s32[2]{0:T(128)} %get-tuple-element.132.src_ref, ...), custom_call_target="tpu_custom_call" | custom-call | flops 3221225472 | bytes 17301504 | tf_op jit(solution)/shard_map/attn_forward/pallas_call | solution.py:358
  208.2 20.9 %ffn_forward.3 = (bf16[512,768]{1,0:T(8,128)(2,1)}, bf16[512,3072]{1,0:T(8,128)(2,1)}, bf16[512,768]{1,0:T(8,128)(2,1)}, bf16[128,512]{1,0:T(8,128)(2,1)}, f32[5...) custom-call(s32[2]{0:T(128)} %pad_add_fusion.4.src_ref, bf16[512,768]{1,0:T(8,128)(2,1)} %get-tuple-element.50.x_ref, ...), custom_call_target="tpu_custom_call" | custom-call | flops 4831838208 | bytes 15728640 | tf_op jit(solution)/shard_map/ffn_forward/pallas_call | solution.py:241
  229.1 14.8 %ffn_backward.2 = (bf16[512,768]{1,0:T(8,128)(2,1)}, bf16[144,768]{1,0:T(8,128)(2,1)}) custom-call(s32[2]{0:T(128)} %pad_add_fusion.4.src_ref, bf16[512,768]{1,0:T(8,128)(2,1)} %pad_maximum_fusion.7.dy_ref, bf16[512,768]{1,0:T(8,128)(2,1)} %get-tuple-element.52.rest_0_, bf16[128,512]{1,0:T(8,128)(2,1)} %get-tuple-element.53.rest_1_, ...), custom_call_target="tpu_custom_call" | custom-call | flops 4831838208 | bytes 15728640 | tf_op jit(solution)/shard_map/ffn_backward/pallas_call | solution.py:289
  244.0 20.1 %attn_backward.2 = (bf16[512,768]{1,0:T(8,128)(2,1)}, bf16[144,768]{1,0:T(8,128)(2,1)}) custom-call(s32[2]{0:T(128)} %get-tuple-element.132.src_ref, bf16[512,768]{1,0:T(8,128)(2,1)} %get-tuple-element.58.dy_ref, bf16[512,768]{1,0:T(8,128)(2,1)} %get-tuple-element.59.rest_0_, bf16[128,512]{1,0:T(8,128)(2,1)} %get-tuple-element.60.rest_1_, ...), custom_call_target="tpu_custom_call" | custom-call | flops 4026531840 | bytes 17301504 | tf_op jit(solution)/shard_map/attn_backward/pallas_call | solution.py:438
  264.1 14.8 %ffn_backward.3 = (bf16[512,768]{1,0:T(8,128)(2,1)}, bf16[144,768]{1,0:T(8,128)(2,1)}) custom-call(s32[2]{0:T(128)} %get-tuple-element.131.src_ref, bf16[512,768]{1,0:T(8,128)(2,1)} %get-tuple-element.67.dy_ref, bf16[512,768]{1,0:T(8,128)(2,1)} %get-tuple-element.68.rest_0_, bf16[128,512]{1,0:T(8,128)(2,1)} %get-tuple-element.69.rest_1_, ...), custom_call_target="tpu_custom_call" | custom-call | flops 4831838208 | bytes 15728640 | tf_op jit(solution)/shard_map/ffn_backward/pallas_call | solution.py:289
  278.9 19.9 %attn_backward.3 = (bf16[512,768]{1,0:T(8,128)(2,1)}, bf16[144,768]{1,0:T(8,128)(2,1)}) custom-call(s32[2]{0:T(128)} %pad_add_fusion.1.src_ref, bf16[512,768]{1,0:T(8,128)(2,1)} %get-tuple-element.74.dy_ref, bf16[512,768]{1,0:T(8,128)(2,1)} %get-tuple-element.75.rest_0_, bf16[128,512]{1,0:T(8,128)(2,1)} %get-tuple-element.76.rest_1_, ...), custom_call_target="tpu_custom_call" | custom-call | flops 4026531840 | bytes 17301504 | tf_op jit(solution)/shard_map/attn_backward/pallas_call | solution.py:438
  298.9 1.2 pad_maximum_fusion.5
  300.2 1.6 collective-permute-start.16
  301.8 1.4 pad_maximum_fusion.2
  303.3 1.4 slice_bitcast_fusion.2
  304.6 7.7 %collective-permute-done.16 = bf16[2,144,768]{2,1,0:T(8,128)(2,1)S(1)} collective-permute-done((bf16[2,144,768]{2,1,0:T(8,128)(2,1)S(1)}, bf16[2,144,768]{2,1,0:T(8,128)(2,1)S(1)}, u32[]{:S(2)}, u32[]{:S(2)}) %collective-permute-start.16) | collective-permute-done | bytes 442400 | tf_op jit(solution)/shard_map/ppermute | solution.py:473
  312.5 1.3 collective-permute-start.17
  313.8 0.4 pad_maximum_fusion
  314.3 4.9 %collective-permute-done.17 = bf16[1,144,768]{2,1,0:T(8,128)(2,1)S(1)} collective-permute-done((bf16[1,144,768]{2,1,0:T(8,128)(2,1)S(1)}, bf16[1,144,768]{2,1,0:T(8,128)(2,1)S(1)}, u32[]{:S(2)}, u32[]{:S(2)}) %collective-permute-start.17) | collective-permute-done | bytes 221216 | tf_op jit(solution)/shard_map/ppermute | solution.py:473
  319.3 1.4 slice_bitcast_fusion.3
  320.7 0.5 collective-permute-start.7
  321.2 1.6 collective-permute-start.19
  322.9 5.9 %collective-permute-done.19 = bf16[144,768]{1,0:T(8,128)(2,1)} collective-permute-done((bf16[144,768]{1,0:T(8,128)(2,1)S(1)}, bf16[144,768]{1,0:T(8,128)(2,1)}, u32[]{:S(2)}, u32[]{:S(2)}) %collective-permute-start.19) | collective-permute-done | bytes 221216 | tf_op jit(solution)/shard_map/ppermute | solution.py:476
  328.7 1.0 add_convert_fusion.2
  329.7 2.7 collective-permute-start.20
  332.4 2.2 maximum_select_fusion.1
  334.9 1.8 collective-permute-start.13
  336.7 5.3 %collective-permute-done.20 = bf16[144,768]{1,0:T(8,128)(2,1)S(1)} collective-permute-done((bf16[144,768]{1,0:T(8,128)(2,1)S(1)}, bf16[144,768]{1,0:T(8,128)(2,1)S(1)}, u32[]{:S(2)}, u32[]{:S(2)}) %collective-permute-start.20) | collective-permute-done | bytes 221216 | tf_op jit(solution)/shard_map/ppermute | solution.py:476
  342.0 1.5 collective-permute-start.14
  343.5 1.8 collective-permute-start.15
  345.3 2.3 maximum_select_fusion
  348.2 1.4 collective-permute-start.9
  349.6 5.8 %collective-permute-done.13 = bf16[2,256,768]{2,1,0:T(8,128)(2,1)S(1)} collective-permute-done((bf16[2,256,768]{2,1,0:T(8,128)(2,1)S(1)}, bf16[2,256,768]{2,1,0:T(8,128)(2,1)S(1)}, u32[]{:S(2)}, u32[]{:S(2)}) %collective-permute-start.13) | collective-permute-done | bytes 786464 | tf_op jit(solution)/shard_map/ppermute | solution.py:473
  355.4 1.4 collective-permute-start.10
  356.8 0.6 fusion.5
  357.4 0.5 slice.87
  357.9 0.8 slice_bitcast_fusion.4
  358.7 20.7 %collective-permute-done.14 = bf16[2,256,768]{2,1,0:T(8,128)(2,1)S(1)} collective-permute-done((bf16[2,256,768]{2,1,0:T(8,128)(2,1)S(1)}, bf16[2,256,768]{2,1,0:T(8,128)(2,1)S(1)}, u32[]{:S(2)}, u32[]{:S(2)}) %collective-permute-start.14) | collective-permute-done | bytes 786464 | tf_op jit(solution)/shard_map/ppermute | solution.py:473
  379.4 0.4 pad_maximum_fusion.3
  380.0 9.1 %collective-permute-done.8 = bf16[2,256,768]{2,1,0:T(8,128)(2,1)S(1)} collective-permute-done((bf16[2,256,768]{2,1,0:T(8,128)(2,1)S(1)}, bf16[2,256,768]{2,1,0:T(8,128)(2,1)S(1)}, u32[]{:S(2)}, u32[]{:S(2)}) %collective-permute-start.8) | collective-permute-done | bytes 786464 | tf_op jit(solution)/shard_map/ppermute | solution.py:473
  389.2 21.8 %collective-permute-done.9 = bf16[2,256,768]{2,1,0:T(8,128)(2,1)S(1)} collective-permute-done((bf16[2,256,768]{2,1,0:T(8,128)(2,1)S(1)}, bf16[2,256,768]{2,1,0:T(8,128)(2,1)S(1)}, u32[]{:S(2)}, u32[]{:S(2)}) %collective-permute-start.9) | collective-permute-done | bytes 786464 | tf_op jit(solution)/shard_map/ppermute | solution.py:473
  411.7 1.9 maximum_bitcast_fusion.1
  413.5 1.9 maximum_bitcast_fusion
  (63 shorter events, 2.5 us)
Async XLA Ops:
  7.7 59.3 %collective-permute-start.1 = (bf16[416,3072]{1,0:T(8,128)(2,1)S(1)}, bf16[416,3072]{1,0:T(8,128)(2,1)S(1)}, u32[]{:S(2)}, u32[]{:S(2)}) collective-permute-start(bf16[416,3072]{1,0:T(8,128)(2,1)S(1)} %pad_maximum_fusion.4), channel_id=1, source_target_pairs={{0,8},{8,0},{16,24},{24,16},{1,9},{9,1},{17,25},{25,17},{2,10},{10... | collective-permute-start | bytes 7667720 | tf_op jit(solution)/shard_map/ppermute | solution.py:473
  10.7 111.8 %collective-permute-start.2 = (bf16[416,3072]{1,0:T(8,128)(2,1)S(1)}, bf16[416,3072]{1,0:T(8,128)(2,1)}, u32[]{:S(2)}, u32[]{:S(2)}) collective-permute-start(bf16[416,3072]{1,0:T(8,128)(2,1)S(1)} %pad_maximum_fusion.4), channel_id=1, source_target_pairs={{0,16},{8,24},{16,0},{24,8},{1,17},{9,25},{17,1},{25,9},{2,18},{10... | collective-permute-start | bytes 7667720 | tf_op jit(solution)/shard_map/ppermute | solution.py:473
  12.2 110.3 %collective-permute-start.3 = (bf16[416,3072]{1,0:T(8,128)(2,1)S(1)}, bf16[416,3072]{1,0:T(8,128)(2,1)}, u32[]{:S(2)}, u32[]{:S(2)}) collective-permute-start(bf16[416,3072]{1,0:T(8,128)(2,1)S(1)} %pad_maximum_fusion.4), channel_id=1, source_target_pairs={{0,24},{8,16},{16,8},{24,0},{1,25},{9,17},{17,9},{25,1},{2,26},{10... | collective-permute-start | bytes 7667720 | tf_op jit(solution)/shard_map/ppermute | solution.py:473
  67.0 70.4 %copy-start = (bf16[416,3072]{1,0:T(8,128)(2,1)}, bf16[416,3072]{1,0:T(8,128)(2,1)S(1)}, u32[]{:S(2)}) copy-start(bf16[416,3072]{1,0:T(8,128)(2,1)S(1)} %collective-permute-done.1.rest_0_.rest_8_.rest_10_) | copy-start | bytes 7667716
  67.0 76.6 %collective-permute-start.4 = (bf16[416,3072]{1,0:T(8,128)(2,1)S(1)}, bf16[416,3072]{1,0:T(8,128)(2,1)}, u32[]{:S(2)}, u32[]{:S(2)}) collective-permute-start(bf16[416,3072]{1,0:T(8,128)(2,1)S(1)} %collective-permute-done.1.rest_0_.rest_8_.rest_10_), channel_id=1, source_target_pairs={{0,1},{1,0},{2,3},{3,2},{4,5},{5,4},{6,7},{7,6},{8,9},{9,8},{10,11... | collective-permute-start | bytes 7667720 | tf_op jit(solution)/shard_map/ppermute | solution.py:476
  122.5 21.1 %collective-permute-start.5 = (bf16[416,3072]{1,0:T(8,128)(2,1)}, bf16[416,3072]{1,0:T(8,128)(2,1)}, u32[]{:S(2)}, u32[]{:S(2)}) collective-permute-start(bf16[416,3072]{1,0:T(8,128)(2,1)} %collective-permute-done.2.rest_1_.rest_9_.rest_11_), channel_id=1, source_target_pairs={{0,1},{1,0},{2,3},{3,2},{4,5},{5,4},{6,7},{7,6},{8,9},{9,8},{10,11... | collective-permute-start | bytes 7667720 | tf_op jit(solution)/shard_map/ppermute | solution.py:476
  122.5 21.1 %collective-permute-start.6 = (bf16[416,3072]{1,0:T(8,128)(2,1)}, bf16[416,3072]{1,0:T(8,128)(2,1)}, u32[]{:S(2)}, u32[]{:S(2)}) collective-permute-start(bf16[416,3072]{1,0:T(8,128)(2,1)} %collective-permute-done.3.rest_2_.rest_10_.rest_12_), channel_id=1, source_target_pairs={{0,1},{1,0},{2,3},{3,2},{4,5},{5,4},{6,7},{7,6},{8,9},{9,8},{10,11... | collective-permute-start | bytes 7667720 | tf_op jit(solution)/shard_map/ppermute | solution.py:476
  125.0 14.6 %collective-permute-start = (bf16[256,768]{1,0:T(8,128)(2,1)}, bf16[256,768]{1,0:T(8,128)(2,1)}, u32[]{:S(2)}, u32[]{:S(2)}) collective-permute-start(bf16[256,768]{1,0:T(8,128)(2,1)} %get-tuple-element.113), channel_id=1, source_target_pairs={{0,1},{1,0},{2,3},{3,2},{4,5},{5,4},{6,7},{7,6},{8,9},{9,8},{10,11... | collective-permute-start | bytes 1179656 | tf_op jit(solution)/shard_map/ppermute | solution.py:476
  127.0 14.7 %collective-permute-start.11 = (bf16[256,768]{1,0:T(8,128)(2,1)}, bf16[256,768]{1,0:T(8,128)(2,1)}, u32[]{:S(2)}, u32[]{:S(2)}) collective-permute-start(bf16[256,768]{1,0:T(8,128)(2,1)} %get-tuple-element.101), channel_id=1, source_target_pairs={{0,1},{1,0},{2,3},{3,2},{4,5},{5,4},{6,7},{7,6},{8,9},{9,8},{10,11... | collective-permute-start | bytes 1179656 | tf_op jit(solution)/shard_map/ppermute | solution.py:476
  129.5 8.5 %copy-start.11 = (s32[512]{0:T(512)}, s32[512]{0:T(512)S(1)}, u32[]{:S(2)}) copy-start(s32[512]{0:T(512)S(1)} %pad_add_fusion) | copy-start | bytes 6148
  278.9 20.0 %copy-start.8 = (bf16[144,768]{1,0:T(8,128)(2,1)S(1)}, bf16[144,768]{1,0:T(8,128)(2,1)}, u32[]{:S(2)}) copy-start(bf16[144,768]{1,0:T(8,128)(2,1)} %get-tuple-element.87) | copy-start | bytes 663556
  278.9 20.0 %copy-start.9 = (bf16[144,768]{1,0:T(8,128)(2,1)S(1)}, bf16[144,768]{1,0:T(8,128)(2,1)}, u32[]{:S(2)}) copy-start(bf16[144,768]{1,0:T(8,128)(2,1)} %get-tuple-element.86) | copy-start | bytes 663556
  278.9 20.0 %copy-start.10 = (bf16[144,768]{1,0:T(8,128)(2,1)S(1)}, bf16[144,768]{1,0:T(8,128)(2,1)}, u32[]{:S(2)}) copy-start(bf16[144,768]{1,0:T(8,128)(2,1)} %get-tuple-element.85) | copy-start | bytes 663556
  298.9 2.9 copy-start.4
  298.9 2.9 copy-start.5
  298.9 2.9 copy-start.6
  300.2 12.2 %collective-permute-start.16 = (bf16[2,144,768]{2,1,0:T(8,128)(2,1)S(1)}, bf16[2,144,768]{2,1,0:T(8,128)(2,1)S(1)}, u32[]{:S(2)}, u32[]{:S(2)}) collective-permute-start(bf16[2,144,768]{2,1,0:T(8,128)(2,1)S(1)} %constant_dynamic-slice_fusion.1), channel_id=1, source_target_pairs={{0,16},{8,24},{16,0},{24,8},{1,17},{9,25},{17,1},{25,9},{2,18},{10... | collective-permute-start | bytes 1327112 | tf_op jit(solution)/shard_map/ppermute | solution.py:473
  303.2 10.6 %copy-start.1 = (bf16[512,768]{1,0:T(8,128)(2,1)S(1)}, bf16[512,768]{1,0:T(8,128)(2,1)}, u32[]{:S(2)}) copy-start(bf16[512,768]{1,0:T(8,128)(2,1)} %get-tuple-element.48.x_ref) | copy-start | bytes 2359300
  303.2 10.6 %copy-start.2 = (bf16[512,768]{1,0:T(8,128)(2,1)S(1)}, bf16[512,768]{1,0:T(8,128)(2,1)}, u32[]{:S(2)}) copy-start(bf16[512,768]{1,0:T(8,128)(2,1)} %get-tuple-element.49.x_ref) | copy-start | bytes 2359300
  303.2 10.6 %copy-start.3 = (bf16[512,768]{1,0:T(8,128)(2,1)S(1)}, bf16[512,768]{1,0:T(8,128)(2,1)}, u32[]{:S(2)}) copy-start(bf16[512,768]{1,0:T(8,128)(2,1)} %get-tuple-element.50.x_ref) | copy-start | bytes 2359300
  303.3 10.6 %copy-start.7 = (bf16[512,768]{1,0:T(8,128)(2,1)S(1)}, bf16[512,768]{1,0:T(8,128)(2,1)}, u32[]{:S(2)}) copy-start(bf16[512,768]{1,0:T(8,128)(2,1)} %get-tuple-element.51) | copy-start | bytes 2359300
  304.6 27.8 %collective-permute-start.12 = (bf16[4,256,768]{2,1,0:T(8,128)(2,1)}, bf16[4,256,768]{2,1,0:T(8,128)(2,1)}, u32[]{:S(2)}, u32[]{:S(2)}) collective-permute-start(bf16[4,256,768]{2,1,0:T(8,128)(2,1)} %get-tuple-element.99), channel_id=1, source_target_pairs={{0,1},{1,0},{2,3},{3,2},{4,5},{5,4},{6,7},{7,6},{8,9},{9,8},{10,11... | collective-permute-start | bytes 4718600 | tf_op jit(solution)/shard_map/ppermute | solution.py:476
  312.5 6.6 %collective-permute-start.17 = (bf16[1,144,768]{2,1,0:T(8,128)(2,1)S(1)}, bf16[1,144,768]{2,1,0:T(8,128)(2,1)S(1)}, u32[]{:S(2)}, u32[]{:S(2)}) collective-permute-start(bf16[1,144,768]{2,1,0:T(8,128)(2,1)S(1)} %constant_dynamic-slice_fusion), channel_id=1, source_target_pairs={{0,8},{8,0},{16,24},{24,16},{1,9},{9,1},{17,25},{25,17},{2,10},{10... | collective-permute-start | bytes 663560 | tf_op jit(solution)/shard_map/ppermute | solution.py:473
  319.2 1.9 collective-permute-start.18
  320.7 24.6 %collective-permute-start.7 = (bf16[4,256,768]{2,1,0:T(8,128)(2,1)}, bf16[4,256,768]{2,1,0:T(8,128)(2,1)}, u32[]{:S(2)}, u32[]{:S(2)}) collective-permute-start(bf16[4,256,768]{2,1,0:T(8,128)(2,1)} %get-tuple-element.111), channel_id=1, source_target_pairs={{0,1},{1,0},{2,3},{3,2},{4,5},{5,4},{6,7},{7,6},{8,9},{9,8},{10,11... | collective-permute-start | bytes 4718600 | tf_op jit(solution)/shard_map/ppermute | solution.py:476
  321.2 7.5 %collective-permute-start.19 = (bf16[144,768]{1,0:T(8,128)(2,1)S(1)}, bf16[144,768]{1,0:T(8,128)(2,1)}, u32[]{:S(2)}, u32[]{:S(2)}) collective-permute-start(bf16[144,768]{1,0:T(8,128)(2,1)S(1)} %add_convert_fusion.3), channel_id=1, source_target_pairs={{0,2},{1,3},{2,0},{3,1},{4,6},{5,7},{6,4},{7,5},{8,10},{9,11},{10,... | collective-permute-start | bytes 663560 | tf_op jit(solution)/shard_map/ppermute | solution.py:476
  329.7 12.2 %collective-permute-start.20 = (bf16[144,768]{1,0:T(8,128)(2,1)S(1)}, bf16[144,768]{1,0:T(8,128)(2,1)S(1)}, u32[]{:S(2)}, u32[]{:S(2)}) collective-permute-start(bf16[144,768]{1,0:T(8,128)(2,1)S(1)} %add_convert_fusion.2), channel_id=1, source_target_pairs={{0,4},{1,5},{2,6},{3,7},{4,0},{5,1},{6,2},{7,3},{8,12},{9,13},{10,... | collective-permute-start | bytes 663560 | tf_op jit(solution)/shard_map/ppermute | solution.py:476
  334.9 20.5 %collective-permute-start.13 = (bf16[2,256,768]{2,1,0:T(8,128)(2,1)S(1)}, bf16[2,256,768]{2,1,0:T(8,128)(2,1)S(1)}, u32[]{:S(2)}, u32[]{:S(2)}) collective-permute-start(bf16[2,256,768]{2,1,0:T(8,128)(2,1)S(1)} %get-tuple-element.97), channel_id=1, source_target_pairs={{0,8},{8,0},{16,24},{24,16},{1,9},{9,1},{17,25},{25,17},{2,10},{10... | collective-permute-start | bytes 2359304 | tf_op jit(solution)/shard_map/ppermute | solution.py:473
  342.0 37.4 %collective-permute-start.14 = (bf16[2,256,768]{2,1,0:T(8,128)(2,1)S(1)}, bf16[2,256,768]{2,1,0:T(8,128)(2,1)S(1)}, u32[]{:S(2)}, u32[]{:S(2)}) collective-permute-start(bf16[2,256,768]{2,1,0:T(8,128)(2,1)S(1)} %get-tuple-element.96), channel_id=1, source_target_pairs={{0,16},{8,24},{16,0},{24,8},{1,17},{9,25},{17,1},{25,9},{2,18},{10... | collective-permute-start | bytes 2359304 | tf_op jit(solution)/shard_map/ppermute | solution.py:473
  343.5 35.9 %collective-permute-start.15 = (bf16[2,256,768]{2,1,0:T(8,128)(2,1)S(1)}, bf16[2,256,768]{2,1,0:T(8,128)(2,1)S(1)}, u32[]{:S(2)}, u32[]{:S(2)}) collective-permute-start(bf16[2,256,768]{2,1,0:T(8,128)(2,1)S(1)} %get-tuple-element.95), channel_id=1, source_target_pairs={{0,24},{8,16},{16,8},{24,0},{1,25},{9,17},{17,9},{25,1},{2,26},{10... | collective-permute-start | bytes 2359304 | tf_op jit(solution)/shard_map/ppermute | solution.py:473
  347.8 41.4 %collective-permute-start.8 = (bf16[2,256,768]{2,1,0:T(8,128)(2,1)S(1)}, bf16[2,256,768]{2,1,0:T(8,128)(2,1)S(1)}, u32[]{:S(2)}, u32[]{:S(2)}) collective-permute-start(bf16[2,256,768]{2,1,0:T(8,128)(2,1)S(1)} %get-tuple-element.109), channel_id=1, source_target_pairs={{0,8},{8,0},{16,24},{24,16},{1,9},{9,1},{17,25},{25,17},{2,10},{10... | collective-permute-start | bytes 2359304 | tf_op jit(solution)/shard_map/ppermute | solution.py:473
  348.2 62.8 %collective-permute-start.9 = (bf16[2,256,768]{2,1,0:T(8,128)(2,1)S(1)}, bf16[2,256,768]{2,1,0:T(8,128)(2,1)S(1)}, u32[]{:S(2)}, u32[]{:S(2)}) collective-permute-start(bf16[2,256,768]{2,1,0:T(8,128)(2,1)S(1)} %get-tuple-element.108), channel_id=1, source_target_pairs={{0,16},{8,24},{16,0},{24,8},{1,17},{9,25},{17,1},{25,9},{2,18},{10... | collective-permute-start | bytes 2359304 | tf_op jit(solution)/shard_map/ppermute | solution.py:473
  355.4 55.6 %collective-permute-start.10 = (bf16[2,256,768]{2,1,0:T(8,128)(2,1)S(1)}, bf16[2,256,768]{2,1,0:T(8,128)(2,1)S(1)}, u32[]{:S(2)}, u32[]{:S(2)}) collective-permute-start(bf16[2,256,768]{2,1,0:T(8,128)(2,1)S(1)} %get-tuple-element.107), channel_id=1, source_target_pairs={{0,24},{8,16},{16,8},{24,0},{1,25},{9,17},{17,9},{25,1},{2,26},{10... | collective-permute-start | bytes 2359304 | tf_op jit(solution)/shard_map/ppermute | solution.py:473
where the time goes:
time: 416 us; the launch traced here: 415 us
  waiting for transfers between devices  192 us (46%)
  Pallas kernels  155 us (37%)
  other arithmetic  24.4 us (6%)
  local copies, waits for them, and re-layouts  21.7 us (5%)
  starting transfers between devices  21.6 us (5%)
    ppermute x11, waiting for transfers between devices, sect(): lax.ppermute(x, 'section', [(i, i ^ apart) for i in range(n_section)])  180 us
    pallas_call x2, Pallas kernels, attn_forward(): call(body, outs, specs, scratch, 1, [VMEM] * 3 + [ANY] * (2 + n_buf), 8 *...  43.6 us
    pallas_call x2, Pallas kernels, ffn_forward(): call(body, outs, [VMEM] * len(outs), scratch, 1, [VMEM, ANY, ANY] + [ANY]...  41.9 us
    pallas_call x2, Pallas kernels, attn_backward(): call(body, outs, [VMEM] * 2, scratch, 1, [VMEM] * 8 + [ANY] * (3 + n_buf)...  40.1 us
    pallas_call x2, Pallas kernels, ffn_backward(): call(body, outs, [VMEM] * 2, scratch, 1, [VMEM] * 6 + [ANY] * (3 + n_buf)...  29.6 us
    ppermute x11, starting transfers between devices, sect(): lax.ppermute(x, 'section', [(i, i ^ apart) for i in range(n_section)])  15.7 us
    ppermute x10, waiting for transfers between devices, peer(): return lax.ppermute(x, 'rows', [(i, i ^ apart) for i in range(n_rows)])  11.2 us
  transfers between devices with their start and end apart: 21, of which 10 were waited for; matrix products, arithmetic and copies ran while one was open for 8% of the time, Pallas kernels for 0%

commit v1 on v0

v1 whole, which is shorter than its diff:
```python
import jax
import jax.numpy as jnp
from jax import lax
from jax.experimental import pallas as pl
from jax.experimental.pallas import tpu as pltpu
from jax.sharding import PartitionSpec as P

HEADS = 12
GROUP = 2
PIECES = 2
EXTRA = 32
COST = 1e8
BF = jnp.bfloat16
F32 = jnp.float32
VMEM = pl.BlockSpec(memory_space=pltpu.VMEM)
ANY = pl.BlockSpec(memory_space=pl.ANY)
SMEM = pl.BlockSpec(memory_space=pltpu.SMEM)
LIMIT = 56 * 1024 * 1024


def dot(left, right):
    return jnp.dot(left, right, preferred_element_type=F32)


def dot_t(left, right):
    return lax.dot_general(left, right, (((1,), (1,)), ((), ())), preferred_element_type=F32)


def gelu_pair(x):
    t = 1.0 / (1.0 + 0.23164188 * jnp.abs(x))
    poly = t * (0.127414796 + t * (-0.142248368 + t * (0.710706871 + t * (
        -0.726576014 + t * 0.530702715))))
    bell = jnp.exp(-0.5 * (x * x))
    tail = poly * bell
    phi = jnp.where(x < 0, tail, 1.0 - tail)
    return x * phi, phi + x * (0.3989422804014327 * bell)


def like(shape, dtype=BF):
    return jax.ShapeDtypeStruct(shape, dtype)


def run(body, ins, outs, stacks, scratch, name, micros, nbytes=0):
    ins, outs = list(ins), list(outs)
    made = [isinstance(x, jax.ShapeDtypeStruct) for x in stacks]
    aliases = {}
    kept = 0
    for i, stack in enumerate(stacks):
        if not made[i]:
            aliases[len(ins) + kept] = len(outs) + i
            kept += 1
    arrays = [a for a, _ in ins] + [x for x, m in zip(stacks, made) if not m]
    specs = [sp for _, sp in ins] + [ANY] * kept
    n_in, n_out, n_stack = len(ins), len(outs), len(stacks)

    def wrapped(*refs):
        got_in = refs[:n_in]
        rest = refs[n_in + kept :]
        body(got_in, rest[:n_out], rest[n_out : n_out + n_stack], rest[n_out + n_stack :])

    res = pl.pallas_call(
        wrapped,
        out_shape=[sh for sh, _ in outs] + [like(x.shape, x.dtype) for x in stacks],
        in_specs=specs,
        out_specs=[sp for _, sp in outs] + [ANY] * n_stack,
        scratch_shapes=scratch,
        name=name,
        input_output_aliases=aliases,
        cost_estimate=pl.CostEstimate(flops=int(micros * COST), bytes_accessed=nbytes,
                                      transcendentals=0),
        compiler_params=pltpu.CompilerParams(vmem_limit_bytes=LIMIT),
    )(*arrays)
    return tuple(res[:n_out]), tuple(res[n_out:])


class Weights:
    def __init__(self, ins, scratch):
        self.src, self.own, self.own_pack = ins[:3]
        self.bufs = ins[3:]
        self.slab, self.pack, self.sem = scratch
        self.rows = self.own.shape[0] // (GROUP * PIECES)

    def start(self):
        sources = len(self.bufs) // PIECES
        size = self.own_pack.shape[0]

        @pl.when(self.src[GROUP] == 0)
        def _():
            pltpu.make_async_copy(self.own_pack, self.pack, self.sem.at[0]).start()

        for i in range(sources // 2):
            @pl.when(self.src[GROUP] == i + 1)
            def _():
                pltpu.make_async_copy(self.bufs[i * PIECES + PIECES - 1].at[pl.ds(self.rows, size)],
                                      self.pack, self.sem.at[0]).start()

        for h in range(GROUP):
            for k in range(PIECES):
                rows = pl.ds((h * PIECES + k) * self.rows, self.rows)

                @pl.when(self.src[h] == 0)
                def _():
                    pltpu.make_async_copy(
                        self.own.at[rows], self.slab.at[rows], self.sem.at[1]).start()

                for i in range(sources):
                    @pl.when(self.src[h] == i + 1)
                    def _():
                        pltpu.make_async_copy(self.bufs[i * PIECES + k].at[pl.ds(0, self.rows)],
                                              self.slab.at[rows], self.sem.at[1]).start()

    def wait_slab(self):
        pltpu.make_async_copy(self.own, self.slab, self.sem.at[1]).wait()

    def wait_pack(self):
        pltpu.make_async_copy(self.own_pack, self.pack, self.sem.at[0]).wait()

    def adapters(self, width, adapt):
        rows = [self.pack[:EXTRA, i * width : (i + 1) * width] for i in range(2 * adapt // EXTRA)]
        zeros = jnp.zeros((128 - adapt, width), BF)
        per = adapt // EXTRA
        down_t = jnp.concatenate(rows[:per] + [zeros], axis=0)
        up = jnp.concatenate(rows[per:] + [zeros], axis=0)
        return down_t, up

    def small(self, i, width):
        low = EXTRA + 2 * i
        return (self.pack[low : low + 1, :width].astype(F32)
                + self.pack[low + 1 : low + 2, :width].astype(F32))


def weight_ins(weights):
    src, own, own_pack, bufs = weights
    return [(src, SMEM), (own, ANY), (own_pack, ANY)] + [(x, ANY) for x in bufs]


def weight_scratch(weights):
    return [pltpu.VMEM(weights[1].shape, BF), pltpu.VMEM(weights[2].shape, BF),
            pltpu.SemaphoreType.DMA((2,))]


def send_out(value_ref, apart, outs, sem):
    half = value_ref.shape[0] // GROUP
    for d in range(len(outs) // GROUP):
        @pl.when(apart == d)
        def _():
            for i in range(GROUP):
                pltpu.make_async_copy(value_ref.at[pl.ds(i * half, half)], outs[GROUP * d + i],
                                      sem).start()

    def wait():
        for i in range(GROUP):
            pltpu.make_async_copy(value_ref.at[pl.ds(i * half, half)], outs[i], sem).wait()
    return wait


def post_forward(wts, x_ref, b_ref, y_ref, saved, adapt):
    low_ref, ut_ref, slope_ref, zhat_ref, rstd_ref = saved
    rows, width = x_ref.shape
    wts.wait_pack()
    down_t, up = wts.adapters(width, adapt)
    down_bias, up_bias, gain, bias = [wts.small(i, width) for i in range(4)]
    step = 128

    def body(i, carry):
        at = pl.ds(pl.multiple_of(i * step, step), step)
        branch = b_ref[at, :]
        low = branch.astype(BF)
        low_ref[at, :] = low
        pre = dot_t(low, down_t) + down_bias[:, :128]
        inner, slope = gelu_pair(pre)
        slope_ref[at, :] = slope
        ut_ref[:, at] = inner.T.astype(BF)
        mixed = x_ref[at, :].astype(F32) + branch + dot(inner.astype(BF), up) + up_bias
        center = mixed - jnp.mean(mixed, axis=-1, keepdims=True)
        rstd = lax.rsqrt(jnp.mean(center * center, axis=-1, keepdims=True) + 1e-05)
        zhat = center * rstd
        y_ref[at, :] = (zhat * gain + bias).astype(BF)
        zhat_ref[at, :] = zhat.astype(BF)
        rstd_ref[at, :] = jnp.broadcast_to(rstd, (step, 128))
        return carry

    lax.fori_loop(0, rows // step, body, 0)


def post_backward(wts, dy_ref, saved, dz_ref, db_ref, grads_ref, dpt_ref, adapt):
    low_ref, ut_ref, slope_ref, zhat_ref, rstd_ref = saved
    rows, width = dy_ref.shape
    wts.wait_pack()
    down_t, up = wts.adapters(width, adapt)
    gain = wts.small(2, width)
    step = 128

    def fold(v):
        return jnp.sum(v.reshape(v.shape[0] // 8, 8, v.shape[1]), axis=0)

    def body(i, carry):
        s_bias, s_gain, s_upb, s_downb = carry
        at = pl.ds(pl.multiple_of(i * step, step), step)
        d_out = dy_ref[at, :].astype(F32)
        zhat = zhat_ref[at, :].astype(F32)
        s_bias = s_bias + fold(d_out)
        s_gain = s_gain + fold(d_out * zhat)
        dz = d_out * gain
        dz = rstd_ref[at, :1] * (dz - jnp.mean(dz, axis=-1, keepdims=True)
                                 - zhat * jnp.mean(dz * zhat, axis=-1, keepdims=True))
        s_upb = s_upb + fold(dz)
        low = dz.astype(BF)
        db_ref[at, :] = low
        d_pre = dot_t(low, up) * slope_ref[at, :]
        s_downb = s_downb + fold(d_pre)
        dpt_ref[:, at] = d_pre.T.astype(BF)
        dz_ref[at, :] = dz
        return s_bias, s_gain, s_upb, s_downb

    zero = jnp.zeros((8, width), F32)
    s_bias, s_gain, s_upb, s_downb = lax.fori_loop(
        0, rows // step, body, (zero, zero, zero, jnp.zeros((8, 128), F32)))
    g_down = dot(dpt_ref[...], low_ref[...])
    g_up = dot(ut_ref[...], db_ref[...])
    grads_ref[0:adapt, :] = g_down[:adapt].astype(BF)
    grads_ref[adapt : 2 * adapt, :] = g_up[:adapt].astype(BF)
    tail = jnp.concatenate(
        [jnp.sum(v, axis=0, keepdims=True) for v in (s_upb, s_gain, s_bias)]
        + [jnp.concatenate([jnp.sum(s_downb, axis=0, keepdims=True),
                            jnp.zeros((1, width - 128), F32)], axis=1),
           jnp.zeros((EXTRA - 4, width), F32)], axis=0)
    grads_ref[2 * adapt :, :] = tail.astype(BF)

    def body2(i, carry):
        at = pl.ds(pl.multiple_of(i * step, step), step)
        d_pre = dpt_ref[:, at].astype(F32).T.astype(BF)
        db_ref[at, :] = (dz_ref[at, :] + dot(d_pre, down_t)).astype(BF)
        return carry

    lax.fori_loop(0, rows // step, body2, 0)


def saved_outs(rows, width):
    return [(like((rows, width)), VMEM), (like((128, rows)), VMEM), (like((rows, 128), F32), VMEM),
            (like((rows, width)), VMEM), (like((rows, 128), F32), VMEM)]


def ffn_forward(x, block, weights, down, adapt, stacks):
    rows, width = x.shape
    ff = weights[1].shape[1]
    chunk = 512
    n_w = len(weight_ins(weights))

    def body(ins, outs, stack_refs, scratch):
        x_ref, down_ref = ins[n_w:]
        y_ref, act_ref, *saved = outs
        down_v, acc, sems = scratch[3:]
        wts = Weights(ins[:n_w], scratch[:3])
        wts.start()
        copy = pltpu.make_async_copy(down_ref.at[block // 2], down_v, sems.at[0])
        copy.start()
        wts.wait_slab()
        copy.wait()

        def step(j, carry):
            cols = pl.ds(pl.multiple_of(j * chunk, chunk), chunk)
            act, slope = gelu_pair(dot(x_ref[...], wts.slab[:, cols]))
            act_ref[:, cols] = slope.astype(BF)
            part = dot(act.astype(BF), down_v[cols, :])

            @pl.when(j == 0)
            def _():
                acc[...] = part

            @pl.when(j > 0)
            def _():
                acc[...] += part
            return carry

        lax.fori_loop(0, ff // chunk, step, 0)
        post_forward(wts, x_ref, acc, y_ref, saved, adapt)
        send_out(y_ref, ins[0][GROUP], stack_refs, sems.at[1])()

    outs = [(like((rows, width)), VMEM), (like((rows, ff)), VMEM)] + saved_outs(rows, width)
    scratch = weight_scratch(weights) + [
        pltpu.VMEM((ff, width), BF), pltpu.VMEM((rows, width), F32),
        pltpu.SemaphoreType.DMA((2,))]
    res, stacks = run(body, weight_ins(weights) + [(x, VMEM), (down, ANY)], outs, stacks, scratch,
                      "ffn_forward", 20)
    return res[0], res[1:], stacks


def ffn_backward(dy, saved, block, weights, down, adapt, stacks):
    rows, width = dy.shape
    ff = weights[1].shape[1]
    chunk = 512
    n_w = len(weight_ins(weights))
    act, saved = saved[0], saved[1:]

    def body(ins, outs, stack_refs, scratch):
        dy_ref, act_ref, down_ref, *saved_ref = ins[n_w:]
        (dx_ref,) = outs
        down_v, act_v, acc, db, dpt, grads, sems = scratch[3:]
        wts = Weights(ins[:n_w], scratch[:3])
        wts.start()
        copy_down = pltpu.make_async_copy(down_ref.at[block // 2], down_v, sems.at[0])
        copy_down.start()
        copy_act = pltpu.make_async_copy(act_ref, act_v, sems.at[1])
        copy_act.start()
        post_backward(wts, dy_ref, saved_ref, acc, db, grads, dpt, adapt)
        copy_grads = pltpu.make_async_copy(grads, stack_refs[-1].at[block], sems.at[2])
        copy_grads.start()
        wts.wait_slab()
        copy_down.wait()
        copy_act.wait()

        def step(j, carry):
            cols = pl.ds(pl.multiple_of(j * chunk, chunk), chunk)
            dg = dot_t(db[...], down_v[cols, :])
            df = (dg * act_v[:, cols].astype(F32)).astype(BF)
            acc[...] += dot_t(df, wts.slab[:, cols])
            return carry

        lax.fori_loop(0, ff // chunk, step, 0)
        dx_ref[...] = acc[...].astype(BF)
        send_out(dx_ref, ins[0][GROUP], stack_refs[:-1], sems.at[3])()
        copy_grads.wait()

    scratch = weight_scratch(weights) + [
        pltpu.VMEM((ff, width), BF), pltpu.VMEM((rows, ff), BF), pltpu.VMEM((rows, width), F32),
        pltpu.VMEM((rows, width), BF), pltpu.VMEM((128, rows), BF),
        pltpu.VMEM((2 * adapt + EXTRA, width), BF), pltpu.SemaphoreType.DMA((4,))]
    res, stacks = run(
        body, weight_ins(weights) + [(dy, VMEM), (act, ANY), (down, ANY)] + [(x, VMEM) for x in saved],
        [(like((rows, width)), VMEM)], stacks, scratch, "ffn_backward", 15)
    return res[0], stacks


def attn_forward(x, seg, block, weights, adapt, stacks):
    rows, width = x.shape
    head = width // HEADS
    pairs = HEADS // 2
    cols_step = 256
    n_w = len(weight_ins(weights))

    def body(ins, outs, stack_refs, scratch):
        x_ref, segc_ref, segr_ref = ins[n_w:]
        y_ref, qkv_ref, p_ref, c_ref, *saved = outs
        acc, bias_v, p_v, sems = scratch[3:]
        wts = Weights(ins[:n_w], scratch[:3])
        wts.start()
        bias_v[...] = jnp.where(segc_ref[...] == segr_ref[...], 0.0, -1e30)
        wts.wait_slab()

        def project(j, carry):
            cols = pl.ds(pl.multiple_of(j * cols_step, cols_step), cols_step)
            scale = jnp.where(j < width // cols_step, head ** -0.5, 1.0)
            qkv_ref[:, cols] = (dot(x_ref[...], wts.slab[:, cols]) * scale).astype(BF)
            return carry

        lax.fori_loop(0, 3 * width // cols_step, project, 0)
        lower = lax.broadcasted_iota(jnp.int32, (rows, 2 * head), 1) < head

        def attend(i, carry):
            def cols_of(part):
                return pl.ds(pl.multiple_of(part * width + i * 2 * head, 2 * head), 2 * head)

            q, k, v = qkv_ref[:, cols_of(0)], qkv_ref[:, cols_of(1)], qkv_ref[:, cols_of(2)]
            parts = []
            for h in range(2):
                q_h = jnp.where(lower == (h == 0), q, jnp.zeros_like(q))
                s = dot_t(q_h, k) + bias_v[...]
                e = jnp.exp(s - jnp.max(s, axis=-1, keepdims=True))
                p = (e * (1.0 / jnp.sum(e, axis=-1, keepdims=True))).astype(BF)
                p_v[2 * i + h] = p
                pltpu.make_async_copy(p_v.at[2 * i + h], p_ref.at[2 * i + h], sems.at[0]).start()
                parts.append(dot(p, v))
            c_ref[:, pl.ds(pl.multiple_of(i * 2 * head, 2 * head), 2 * head)] = jnp.where(
                lower, parts[0], parts[1]).astype(BF)
            return carry

        lax.fori_loop(0, pairs, attend, 0)

        def output(j, carry):
            cols = pl.ds(pl.multiple_of(j * cols_step, cols_step), cols_step)
            acc[:, cols] = dot(c_ref[...], wts.slab[:, pl.ds(
                pl.multiple_of(3 * width + j * cols_step, cols_step), cols_step)])
            return carry

        lax.fori_loop(0, width // cols_step, output, 0)
        post_forward(wts, x_ref, acc, y_ref, saved, adapt)
        send_out(y_ref, ins[0][GROUP], stack_refs, sems.at[1])()
        pltpu.make_async_copy(p_v, p_ref, sems.at[0]).wait()

    outs = [(like((rows, width)), VMEM), (like((rows, 3 * width)), VMEM),
            (like((HEADS, rows, rows)), ANY), (like((rows, width)), VMEM)]
    outs += saved_outs(rows, width)
    scratch = weight_scratch(weights) + [
        pltpu.VMEM((rows, width), F32), pltpu.VMEM((rows, rows), F32),
        pltpu.VMEM((HEADS, rows, rows), BF), pltpu.SemaphoreType.DMA((2,))]
    res, stacks = run(
        body, weight_ins(weights) + [(x, VMEM), (seg[:, None], VMEM), (seg[None, :], VMEM)],
        outs, stacks, scratch, "attn_forward", 20)
    return res[0], res[1:], stacks


def attn_backward(dy, saved, block, weights, adapt, stacks):
    rows, width = dy.shape
    head = width // HEADS
    pairs = HEADS // 2
    cols_step = 256
    n_w = len(weight_ins(weights))
    qkv, probs, ctx = saved[:3]
    saved = saved[3:]

    def body(ins, outs, stack_refs, scratch):
        dy_ref, p_ref, qkv_ref, c_ref, *saved_ref = ins[n_w:]
        p_v, dz, db, dpt, dc_v, dqkv, dx_v, grads, sems = scratch[3:]
        wts = Weights(ins[:n_w], scratch[:3])
        wts.start()
        copy_p = pltpu.make_async_copy(p_ref, p_v, sems.at[0])
        copy_p.start()
        post_backward(wts, dy_ref, saved_ref, dz, db, grads, dpt, adapt)
        copy_grads = pltpu.make_async_copy(grads, stack_refs[-1].at[block], sems.at[1])
        copy_grads.start()
        wts.wait_slab()

        def context(j, carry):
            cols = pl.ds(pl.multiple_of(j * cols_step, cols_step), cols_step)
            dc_v[:, cols] = dot_t(db[...], wts.slab[cols, 3 * width :]).astype(BF)
            return carry

        lax.fori_loop(0, width // cols_step, context, 0)
        copy_p.wait()
        lower = lax.broadcasted_iota(jnp.int32, (rows, 2 * head), 1) < head

        def attend(i, carry):
            def cols_of(part):
                return pl.ds(pl.multiple_of(part * width + i * 2 * head, 2 * head), 2 * head)

            q, k, v = qkv_ref[:, cols_of(0)], qkv_ref[:, cols_of(1)], qkv_ref[:, cols_of(2)]
            dc = dc_v[:, cols_of(0)]
            dc_wide = dc.astype(F32)
            prod = dc_wide * c_ref[:, cols_of(0)].astype(F32)
            q_t = q.astype(F32).T.astype(BF)
            dc_t = dc_wide.T.astype(BF)
            dq, dk, dv = [], [], []
            for h in range(2):
                mine = lower == (h == 0)
                p = p_v[2 * i + h]
                delta = jnp.sum(jnp.where(mine, prod, 0.0), axis=-1, keepdims=True)
                dp = dot_t(jnp.where(mine, dc, jnp.zeros_like(dc)), v)
                ds = (p.astype(F32) * (dp - delta)).astype(BF)
                dq.append(dot(ds, k))
                dk.append(dot(q_t[h * head : (h + 1) * head], ds))
                dv.append(dot(dc_t[h * head : (h + 1) * head], p))
            dqkv[:, cols_of(0)] = (jnp.where(lower, dq[0], dq[1]) * head ** -0.5).astype(BF)
            dqkv[:, cols_of(1)] = jnp.concatenate(dk, axis=0).T.astype(BF)
            dqkv[:, cols_of(2)] = jnp.concatenate(dv, axis=0).T.astype(BF)
            return carry

        lax.fori_loop(0, pairs, attend, 0)

        def output(j, carry):
            cols = pl.ds(pl.multiple_of(j * cols_step, cols_step), cols_step)
            dx_v[:, cols] = (dz[:, cols] + dot_t(dqkv[...], wts.slab[cols, : 3 * width])).astype(BF)
            return carry

        lax.fori_loop(0, width // cols_step, output, 0)
        if outs:
            outs[0][...] = dx_v[...]
        send_out(dx_v, ins[0][GROUP], stack_refs[:-1], sems.at[2])()
        copy_grads.wait()

    outs = [] if block == 0 else [(like((rows, width)), VMEM)]
    scratch = weight_scratch(weights) + [
        pltpu.VMEM((HEADS, rows, rows), BF), pltpu.VMEM((rows, width), F32),
        pltpu.VMEM((rows, width), BF), pltpu.VMEM((128, rows), BF), pltpu.VMEM((rows, width), BF),
        pltpu.VMEM((rows, 3 * width), BF), pltpu.VMEM((rows, width), BF),
        pltpu.VMEM((2 * adapt + EXTRA, width), BF), pltpu.SemaphoreType.DMA((3,))]
    res, stacks = run(
        body, weight_ins(weights) + [(dy, VMEM), (probs, ANY), (qkv, VMEM), (ctx, VMEM)]
        + [(x, VMEM) for x in saved],
        outs, stacks, scratch, "attn_backward", 20)
    return (res[0] if outs else None), stacks


def place_rows(place, pieces):
    count = len(pieces)

    def body(ins, outs, stack_refs, scratch):
        place_ref, pieces_ref = ins[0], ins[1:]
        buf, sems = scratch
        for i, piece in enumerate(pieces_ref):
            pltpu.make_async_copy(piece, buf.at[i], sems.at[i]).start()
        stores = []
        for i, piece in enumerate(pieces_ref):
            pltpu.make_async_copy(piece, buf.at[i], sems.at[i]).wait()
            stores.append(pltpu.make_async_copy(buf.at[i], outs[0].at[place_ref[i]], sems.at[i]))
            stores[-1].start()
        for copy in stores:
            copy.wait()

    res, _ = run(body, [(place, SMEM)] + [(x, ANY) for x in pieces],
                 [(like((count,) + pieces[0].shape), ANY)], [],
                 [pltpu.VMEM((count,) + pieces[0].shape, BF), pltpu.SemaphoreType.DMA((count,))],
                 "place_rows", 3)
    return res[0]


def split_rows(v):
    high = v.astype(BF)
    return high, (v - high.astype(F32)).astype(BF)


def pack_adapters(ad_down, down_bias, ad_up, up_bias, gain, bias):
    width, adapt = ad_down.shape
    rows = []
    for v in (jnp.pad(down_bias, (0, width - adapt)), up_bias, gain, bias):
        rows += list(split_rows(v))
    mats = jnp.concatenate([ad_down.T, ad_up], axis=0).astype(BF)
    mats = jnp.concatenate([mats[i : i + EXTRA] for i in range(0, 2 * adapt, EXTRA)], axis=1)
    rows = jnp.pad(jnp.stack(rows), ((0, 16 - len(rows)), (0, mats.shape[1] - width)))
    return jnp.concatenate([mats, rows], axis=0)


def per_device(tokens, cotangent, segment_ids, slabs, ffn_down,
               ad_down, ad_down_bias, ad_up, ad_up_bias, ln_gain, ln_bias):
    n_section = lax.axis_size("section")
    n_rows = lax.axis_size("rows")
    s = lax.axis_index("section")
    r = lax.axis_index("rows")
    core = r % GROUP
    n_micro, rows_dev, width = tokens.shape
    adapt = ad_down.shape[2]

    def sect(x, apart, to=None):
        pairs = [(i, i ^ apart) for i in range(n_section)]
        return lax.ppermute(x, "section", [p for p in pairs if to is None or p[1] in to])

    def peer(x, apart=1):
        return lax.ppermute(x, "rows", [(i, i ^ apart) for i in range(n_rows)])

    def cross(x, moves):
        pairs = []
        for (s0, c0), (s1, c1) in moves:
            for g in range(n_rows // GROUP):
                pairs.append((s0 * n_rows + g * GROUP + c0, s1 * n_rows + g * GROUP + c1))
        return lax.ppermute(x, ("section", "rows"), pairs)

    own_micro = s * GROUP + core
    peer_micro = s * GROUP + 1 - core

    slab = slabs[0]
    piece = slab.shape[0] // (GROUP * PIECES)
    adapters = (ad_down[0], ad_down_bias[0], ad_up[0], ad_up_bias[0], ln_gain[0], ln_bias[0])
    near, far, passed = [], [], []
    for k in range(PIECES):
        given = lax.dynamic_slice_in_dim(slab, (core * PIECES + k) * piece, piece, 0)
        if k == PIECES - 1:
            own_pack = pack_adapters(*adapters)
            given = jnp.concatenate([given, own_pack], axis=0)
        near.append(sect(given, 1))
        far.append(sect(given, 2))

    def gather_item(x):
        mine = lax.dynamic_index_in_dim(x, own_micro, 0, keepdims=False)
        given = lax.dynamic_index_in_dim(x, peer_micro, 0, keepdims=False)
        return jnp.concatenate([mine, peer(given)], axis=0)

    hidden = gather_item(tokens)
    cot = gather_item(cotangent)
    seg_a = lax.dynamic_slice(segment_ids, (own_micro, r * rows_dev), (1, rows_dev))[0]
    seg_b = lax.dynamic_slice(segment_ids, (own_micro, (r ^ 1) * rows_dev), (1, rows_dev))[0]
    seg = jnp.concatenate([seg_a, seg_b])

    diag, near_x, far_x, diag_x = [], [], [], []
    sections = range(n_section)
    moves = [((t ^ 1, 0), (t, 0)) for t in sections] + [((t ^ 2, 1), (t, 1)) for t in sections]
    for k in range(PIECES):
        near_x.append(peer(near[k]))
        far_x.append(peer(far[k]))
        diag.append(cross(jnp.where(core == 0, far[k], near[k]), moves))
        diag_x.append(peer(diag[k]))

    def weights_of(b):
        d = s ^ b
        src = [jnp.where(d == 0, 0, jnp.where(core == h, d, d + n_section - 1))
               for h in range(GROUP)] + [d]
        return (jnp.stack(src).astype(jnp.int32), slab, own_pack,
                near + far + diag + near_x + far_x + diag_x)

    weights = [weights_of(b) for b in range(n_section)]
    place = jnp.stack([(s ^ d) * GROUP + (core if i == 0 else 1 - core)
                       for d in sections for i in range(GROUP)]).astype(jnp.int32)

    def deliver(pieces, d):
        moves = [((t ^ d, c), (t, 1 - c)) for t in sections for c in range(GROUP)]
        own = pieces[GROUP * d]
        return [own if d == 0 else sect(own, d), cross(pieces[GROUP * d + 1], moves)]

    pieces = tuple([like((rows_dev, width))] * (GROUP * n_section))
    sent, saves = pieces, []
    for b in range(n_section):
        if b % 2 == 0:
            hidden, saved, sent = attn_forward(hidden, seg, b, weights[b], adapt, sent)
        else:
            hidden, saved, sent = ffn_forward(hidden, b, weights[b], ffn_down, adapt, sent)
        saves.append(saved)

    arrived = {3: deliver(sent, 3), 0: deliver(sent, 0)}
    grad = cot
    stacks = pieces + (like((n_section, 2 * adapt + EXTRA, width)),)
    for b in reversed(range(n_section)):
        if b == 2:
            grad, *late = lax.optimization_barrier((grad, *arrived[3], arrived[0][1], *sent))
            arrived[3], arrived[0], sent = late[:2], [arrived[0][0], late[2]], late[3:]
            arrived[1], arrived[2] = deliver(sent, 1), deliver(sent, 2)
        if b == 1:
            grad, *late = lax.optimization_barrier((grad, *arrived[1], *arrived[2]))
            arrived[1], arrived[2] = late[:2], late[2:]
        if b % 2 == 0:
            grad, stacks = attn_backward(grad, saves[b], b, weights[b], adapt, stacks)
        else:
            grad, stacks = ffn_backward(grad, saves[b], b, weights[b], ffn_down, adapt, stacks)

    block_outputs = place_rows(place, [x for d in sections for x in arrived[d]])
    arrived = [deliver(stacks, d) for d in sections]
    total, arrived[0][1] = lax.optimization_barrier((stacks[-1], arrived[0][1]))
    input_grads = place_rows(place, [x for pair in arrived for x in pair])

    part = total.shape[1] // GROUP
    keep = lax.dynamic_slice_in_dim(total, core * part, part, 1)
    give = lax.dynamic_slice_in_dim(total, (1 - core) * part, part, 1)

    def added(left, right):
        return (left.astype(F32) + right.astype(F32)).astype(BF)

    total = added(keep, peer(give))
    apart = n_section // 2
    while apart >= 1:
        high = (s // apart) % 2
        keep = lax.dynamic_slice_in_dim(total, high * apart, apart, 0)
        give = lax.dynamic_slice_in_dim(total, (1 - high) * apart, apart, 0)
        total = added(keep, sect(give, apart))
        apart //= 2
    total = total[0]
    apart = GROUP
    while apart < n_rows:
        total = added(total, peer(total, apart))
        apart *= 2
    other = peer(total)
    total = jnp.where(core == 0, jnp.concatenate([total, other], axis=0),
                      jnp.concatenate([other, total], axis=0)).astype(F32)
    return (block_outputs[None], input_grads[None], total[:adapt].T[None],
            total[2 * adapt + 3, :adapt][None], total[adapt : 2 * adapt][None],
            total[2 * adapt][None], total[2 * adapt + 1][None], total[2 * adapt + 2][None])


def solution(mesh):
    in_specs = (
        P(None, "rows", None), P(None, "rows", None), P(), P("section", None, None), P(),
        P("section", None, None), P("section", None), P("section", None, None),
        P("section", None), P("section", None), P("section", None),
    )
    out_specs = (
        P("section", None, "rows", None), P("section", None, "rows", None),
        P("section", None, None), P("section", None), P("section", None, None),
        P("section", None), P("section", None), P("section", None),
    )
    return jax.shard_map(
        per_device, mesh=mesh, in_specs=in_specs, out_specs=out_specs, check_vma=False
    )
```

time: 416 us -> 348 us (0.84)
  waiting for transfers between devices: 192 us -> 121 us
  Pallas kernels: 155 us -> 167 us
  local copies, waits for them, and re-layouts: 21.7 us -> 12.1 us
  other arithmetic: 24.4 us -> 15.8 us
  starting transfers between devices: 21.6 us -> 29.7 us
    ppermute x11 -> x22, waiting for transfers between devices: 180 us -> 116 us  [the longest x12 80.7 us: sect(): lax.ppermute(x, 'section', [p for p in pairs if to is None or p[1] in to])]
    pallas_call x8 -> x10, Pallas kernels: 155 us -> 167 us  [run(): pl.pallas_call(wrapped, out_shape=[sh for sh, _ in outs] + [like(x.shape,...]
    squeeze x3 -> x0, local copies, waits for them, and re-layouts: 8.33 us -> none  [the longest x1 7.9 us: per_device(): ffn_down[b // 2]]
    ppermute x10 -> x12, waiting for transfers between devices: 11.2 us -> 5.43 us  [peer(): return lax.ppermute(x, 'rows', [(i, i ^ apart) for i in range(n_rows)])]
    ppermute x11 -> x22, starting transfers between devices: 15.7 us -> 20.5 us  [the longest x12 16.6 us: sect(): lax.ppermute(x, 'section', [p for p in pairs if to is None or p[1] in to])]
    another operation x11 -> x4, other arithmetic: 7.41 us -> 2.71 us  [the longest x3 1.77 us: weights_of(): jnp.stack(src).astype(jnp.int32)]
    ppermute x10 -> x12, starting transfers between devices: 5.89 us -> 9.18 us  [peer(): return lax.ppermute(x, 'rows', [(i, i ^ apart) for i in range(n_rows)])]
  transfers between devices with their start and end apart: 21 -> 34, of which waited for: 10 -> 17; matrix products, arithmetic and copies ran while one was open for 8% -> 4% of each run, Pallas kernels for 0% -> 38%
where the time goes in v1:
time: 348 us; the launch traced here: 347 us
  Pallas kernels  167 us (48%)
  waiting for transfers between devices  121 us (35%)
  starting transfers between devices  29.7 us (9%)
  other arithmetic  15.8 us (5%)
  local copies, waits for them, and re-layouts  12.1 us (3%)
    pallas_call x10, Pallas kernels, run(): pl.pallas_call(wrapped, out_shape=[sh for sh, _ in outs] + [like(x.shape,...  167 us
    ppermute x12, waiting for transfers between devices, sect(): lax.ppermute(x, 'section', [p for p in pairs if to is None or p[1] in to])  80.7 us
    ppermute x10, waiting for transfers between devices, cross(): return lax.ppermute(x, ('section', 'rows'), pairs)  35.1 us
    ppermute x12, starting transfers between devices, sect(): lax.ppermute(x, 'section', [p for p in pairs if to is None or p[1] in to])  16.6 us
    ppermute x12, starting transfers between devices, peer(): return lax.ppermute(x, 'rows', [(i, i ^ apart) for i in range(n_rows)])  9.18 us
  transfers between devices with their start and end apart: 34, of which 17 were waited for; matrix products, arithmetic and copies ran while one was open for 4% of the time, Pallas kernels for 38%

profile of v1, /device:TPU:0, one launch (start us, length us, event | category | flops | bytes accessed | tf_op | source)
XLA Modules:
  0.0 347.3 jit_solution(10247385934948352056)
XLA Ops:
  2.0 0.8 subtract_convert_fusion.2
  2.7 0.9 convert.10
  3.7 0.9 convert_bitcast_fusion
  4.7 0.8 subtract_convert_fusion
  5.6 2.8 dynamic-slice_bitcast_fusion
  8.4 1.2 pad_maximum_fusion
  9.6 2.9 collective-permute-start.1
  12.5 1.5 collective-permute-start.3
  14.6 31.3 %collective-permute-done.1.refs_4_ = bf16[240,3072]{1,0:T(8,128)(2,1)S(1)} collective-permute-done((bf16[240,3072]{1,0:T(8,128)(2,1)}, bf16[240,3072]{1,0:T(8,128)(2,1)S(1)}, u32[]{:S(2)}, u32[]{:S(2)}) %collective-permute-start.1) | collective-permute-done | bytes 1474592 | tf_op jit(solution)/shard_map/ppermute | solution.py:535
  45.9 2.1 collective-permute-done.3.refs_6_
  48.0 1.4 broadcast_select_fusion
  49.4 21.0 %collective-permute-done.refs_3_ = bf16[192,3072]{1,0:T(8,128)(2,1)} collective-permute-done((bf16[192,3072]{1,0:T(8,128)(2,1)}, bf16[192,3072]{1,0:T(8,128)(2,1)}, u32[]{:S(2)}, u32[]{:S(2)}) %collective-permute-start) | collective-permute-done | bytes 1179680 | tf_op jit(solution)/shard_map/ppermute | solution.py:535
  70.4 2.9 collective-permute-done.2.refs_5_
  73.3 2.4 broadcast_select_fusion.1
  75.8 1.2 dynamic-slice_bitcast_fusion.5
  77.6 1.6 collective-permute-done.12
  80.0 6.3 %collective-permute-done.5.refs_8_ = bf16[240,3072]{1,0:T(8,128)(2,1)} collective-permute-done((bf16[240,3072]{1,0:T(8,128)(2,1)}, bf16[240,3072]{1,0:T(8,128)(2,1)}, u32[]{:S(2)}, u32[]{:S(2)}) %collective-permute-start.5) | collective-permute-done | bytes 1474592 | tf_op jit(solution)/shard_map/ppermute | solution.py:545
  86.2 1.6 collective-permute-start.11
  87.8 11.1 %collective-permute-done.4.refs_7_ = bf16[192,3072]{1,0:T(8,128)(2,1)} collective-permute-done((bf16[192,3072]{1,0:T(8,128)(2,1)}, bf16[192,3072]{1,0:T(8,128)(2,1)}, u32[]{:S(2)}, u32[]{:S(2)}) %collective-permute-start.4) | collective-permute-done | bytes 1179680 | tf_op jit(solution)/shard_map/ppermute | solution.py:545
  98.8 1.3 collective-permute-start.8
  100.1 0.8 fusion.5
  100.9 0.9 copy.70.refs_16_
  103.6 1.2 dynamic-slice_bitcast_fusion.3
  104.8 0.7 pad_maximum_fusion.3.refs_2_
  105.5 0.9 pad_maximum_fusion.1.refs_15_
  107.0 22.6 %attn_forward.2 = (bf16[512,768]{1,0:T(8,128)(2,1)}, bf16[512,2304]{1,0:T(8,128)(2,1)}, bf16[12,512,512]{2,1,0:T(8,128)(2,1)}, bf16[512,768]{1,0:T(8,128)(2,1)},...) custom-call(s32[3]{0:T(128)} %pad_add_fusion.4.refs_0_, ...), custom_call_target="tpu_custom_call" | custom-call | flops 2000000000 | tf_op jit(solution)/shard_map/attn_forward/pallas_call | solution.py:61
  129.6 22.4 %ffn_forward.2 = (bf16[512,768]{1,0:T(8,128)(2,1)}, bf16[512,3072]{1,0:T(8,128)(2,1)}, bf16[512,768]{1,0:T(8,128)(2,1)}, bf16[128,512]{1,0:T(8,128)(2,1)}, f32[5...) custom-call(s32[3]{0:T(128)} %get-tuple-element.266.refs_0_, ...), custom_call_target="tpu_custom_call", output_to_operand_aliasing={{7}: (17, {}), {8}: (18, {}), {9}: (19, {}), {10}: (20, {})... | custom-call | flops 2000000000 | tf_op jit(solution)/shard_map/ffn_forward/pallas_call | solution.py:61
  152.0 22.6 %attn_forward.3 = (bf16[512,768]{1,0:T(8,128)(2,1)}, bf16[512,2304]{1,0:T(8,128)(2,1)}, bf16[12,512,512]{2,1,0:T(8,128)(2,1)}, bf16[512,768]{1,0:T(8,128)(2,1)},...) custom-call(s32[3]{0:T(128)} %get-tuple-element.265.refs_0_, ...), custom_call_target="tpu_custom_call", output_to_operand_aliasing={{9}: (18, {}), {10}: (19, {}), {11}: (20, {}), {12}: (21, {... | custom-call | flops 2000000000 | tf_op jit(solution)/shard_map/attn_forward/pallas_call | solution.py:61
  174.6 22.4 %ffn_forward.3 = (bf16[512,768]{1,0:T(8,128)(2,1)}, bf16[512,3072]{1,0:T(8,128)(2,1)}, bf16[512,768]{1,0:T(8,128)(2,1)}, bf16[128,512]{1,0:T(8,128)(2,1)}, f32[5...) custom-call(s32[3]{0:T(128)} %pad_add_fusion.1.refs_0_, ...), custom_call_target="tpu_custom_call", output_to_operand_aliasing={{7}: (17, {}), {8}: (18, {}), {9}: (19, {}), {10}: (20, {})... | custom-call | flops 2000000000 | tf_op jit(solution)/shard_map/ffn_forward/pallas_call | solution.py:61
  197.0 1.6 collective-permute-start.14
  198.6 0.7 collective-permute-start.15
  199.3 0.8 collective-permute-start.16
  200.1 0.9 pad_maximum_fusion.2.refs_15_
  201.0 15.5 %ffn_backward.2 = (bf16[512,768]{1,0:T(8,128)(2,1)}, bf16[256,768]{1,0:T(8,128)(2,1)}, bf16[256,768]{1,0:T(8,128)(2,1)}, bf16[256,768]{1,0:T(8,128)(2,1)}, bf16[...) custom-call(s32[3]{0:T(128)} %pad_add_fusion.1.refs_0_, ...), custom_call_target="tpu_custom_call" | custom-call | flops 1500000000 | tf_op jit(solution)/shard_map/ffn_backward/pallas_call | solution.py:61
  216.7 1.4 collective-permute-start.17
  218.1 0.8 collective-permute-start.18
  218.9 1.5 collective-permute-start.19
  220.4 20.2 %attn_backward.2 = (bf16[512,768]{1,0:T(8,128)(2,1)}, bf16[256,768]{1,0:T(8,128)(2,1)}, bf16[256,768]{1,0:T(8,128)(2,1)}, bf16[256,768]{1,0:T(8,128)(2,1)}, bf16...) custom-call(s32[3]{0:T(128)} %get-tuple-element.265.refs_0_, ...), custom_call_target="tpu_custom_call", output_to_operand_aliasing={{1}: (24, {}), {2}: (25, {}), {3}: (26, {}), {4}: (27, {}),... | custom-call | flops 2000000000 | tf_op jit(solution)/shard_map/attn_backward/pallas_call | solution.py:61
  240.7 15.8 %ffn_backward.3 = (bf16[512,768]{1,0:T(8,128)(2,1)}, bf16[256,768]{1,0:T(8,128)(2,1)}, bf16[256,768]{1,0:T(8,128)(2,1)}, bf16[256,768]{1,0:T(8,128)(2,1)}, bf16[...) custom-call(s32[3]{0:T(128)} %get-tuple-element.266.refs_0_, ...), custom_call_target="tpu_custom_call", output_to_operand_aliasing={{1}: (23, {}), {2}: (24, {}), {3}: (25, {}), {4}: (26, {}),... | custom-call | flops 1500000000 | tf_op jit(solution)/shard_map/ffn_backward/pallas_call | solution.py:61
  256.5 19.1 %attn_backward.3 = (bf16[256,768]{1,0:T(8,128)(2,1)}, bf16[256,768]{1,0:T(8,128)(2,1)}, bf16[256,768]{1,0:T(8,128)(2,1)}, bf16[256,768]{1,0:T(8,128)(2,1)}, bf16...) custom-call(s32[3]{0:T(128)} %pad_add_fusion.4.refs_0_, ...), custom_call_target="tpu_custom_call", output_to_operand_aliasing={{0}: (24, {}), {1}: (25, {}), {2}: (26, {}), {3}: (27, {}),... | custom-call | flops 2000000000 | tf_op jit(solution)/shard_map/attn_backward/pallas_call | solution.py:61
  275.7 0.7 collective-permute-start.21
  276.3 1.6 collective-permute-done.21.refs_2_
  277.9 1.2 constant_dynamic-slice_fusion.2
  279.6 1.5 collective-permute-done.28
  281.0 1.1 add_convert_fusion
  282.3 1.6 collective-permute-start.29
  283.9 6.8 %collective-permute-done.29 = bf16[2,80,768]{2,1,0:T(8,128)(2,1)} collective-permute-done((bf16[2,80,768]{2,1,0:T(8,128)(2,1)S(1)}, bf16[2,80,768]{2,1,0:T(8,128)(2,1)}, u32[]{:S(2)}, u32[]{:S(2)}) %collective-permute-start.29) | collective-permute-done | bytes 245792 | tf_op jit(solution)/shard_map/ppermute | solution.py:535
  290.7 1.0 add_convert_fusion.1
  291.7 1.0 collective-permute-start.30
  292.8 3.9 %collective-permute-done.30 = bf16[1,80,768]{2,1,0:T(8,128)(2,1)S(1)} collective-permute-done((bf16[1,80,768]{2,1,0:T(8,128)(2,1)S(1)}, bf16[1,80,768]{2,1,0:T(8,128)(2,1)S(1)}, u32[]{:S(2)}, u32[]{:S(2)}) %collective-permute-start.30) | collective-permute-done | bytes 122912 | tf_op jit(solution)/shard_map/ppermute | solution.py:535
  296.7 1.6 collective-permute-start.31
  298.4 1.0 collective-permute-start.22
  299.3 2.3 collective-permute-done.31
  301.7 2.8 collective-permute-start.32
  304.5 1.6 collective-permute-start.24
  306.1 0.8 collective-permute-start.25
  307.5 1.9 collective-permute-start.26
  309.5 6.5 %collective-permute-done.23.refs_4_ = bf16[256,768]{1,0:T(8,128)(2,1)S(1)} collective-permute-done((bf16[256,768]{1,0:T(8,128)(2,1)S(1)}, bf16[256,768]{1,0:T(8,128)(2,1)S(1)}, u32[]{:S(2)}, u32[]{:S(2)}) %collective-permute-start.23) | collective-permute-done | bytes 393248 | tf_op jit(solution)/shard_map/ppermute | solution.py:545
  316.1 0.7 stack.98.refs_0_
  316.8 3.4 place_rows.2
  320.2 12.1 %collective-permute-done.24.refs_5_ = bf16[256,768]{1,0:T(8,128)(2,1)} collective-permute-done((bf16[256,768]{1,0:T(8,128)(2,1)S(1)}, bf16[256,768]{1,0:T(8,128)(2,1)}, u32[]{:S(2)}, u32[]{:S(2)}) %collective-permute-start.24) | collective-permute-done | bytes 393248 | tf_op jit(solution)/shard_map/ppermute | solution.py:535
  332.3 9.6 %collective-permute-done.25.refs_6_ = bf16[256,768]{1,0:T(8,128)(2,1)} collective-permute-done((bf16[256,768]{1,0:T(8,128)(2,1)S(1)}, bf16[256,768]{1,0:T(8,128)(2,1)}, u32[]{:S(2)}, u32[]{:S(2)}) %collective-permute-start.25) | collective-permute-done | bytes 393248 | tf_op jit(solution)/shard_map/ppermute | solution.py:545
  341.9 3.4 place_rows.3
  345.4 0.8 slice_bitcast_fusion
  (112 shorter events, 8.4 us)
Async XLA Ops:
  4.7 3.7 %copy-start.12 = (bf16[32,768]{1,0:T(8,128)(2,1)}, bf16[32,768]{1,0:T(8,128)(2,1)S(1)}, u32[]{:S(2)}) copy-start(bf16[32,768]{1,0:T(8,128)(2,1)S(1)} %get-tuple-element.253) | copy-start | bytes 147460
  4.7 3.7 %copy-start.14 = (bf16[32,768]{1,0:T(8,128)(2,1)}, bf16[32,768]{1,0:T(8,128)(2,1)S(1)}, u32[]{:S(2)}) copy-start(bf16[32,768]{1,0:T(8,128)(2,1)S(1)} %get-tuple-element.254) | copy-start | bytes 147460
  9.6 36.3 %collective-permute-start.1 = (bf16[240,3072]{1,0:T(8,128)(2,1)}, bf16[240,3072]{1,0:T(8,128)(2,1)S(1)}, u32[]{:S(2)}, u32[]{:S(2)}) collective-permute-start(bf16[240,3072]{1,0:T(8,128)(2,1)} %pad_maximum_fusion), channel_id=1, source_target_pairs={{0,8},{8,0},{16,24},{24,16},{1,9},{9,1},{17,25},{25,17},{2,10},{10... | collective-permute-start | bytes 4423688 | tf_op jit(solution)/shard_map/ppermute | solution.py:535
  12.5 35.4 %collective-permute-start.3 = (bf16[240,3072]{1,0:T(8,128)(2,1)}, bf16[240,3072]{1,0:T(8,128)(2,1)S(1)}, u32[]{:S(2)}, u32[]{:S(2)}) collective-permute-start(bf16[240,3072]{1,0:T(8,128)(2,1)} %pad_maximum_fusion), channel_id=1, source_target_pairs={{0,16},{8,24},{16,0},{24,8},{1,17},{9,25},{17,1},{25,9},{2,18},{10... | collective-permute-start | bytes 4423688 | tf_op jit(solution)/shard_map/ppermute | solution.py:535
  14.0 56.4 %collective-permute-start = (bf16[192,3072]{1,0:T(8,128)(2,1)}, bf16[192,3072]{1,0:T(8,128)(2,1)}, u32[]{:S(2)}, u32[]{:S(2)}) collective-permute-start(bf16[192,3072]{1,0:T(8,128)(2,1)} %get-tuple-element.243), channel_id=1, source_target_pairs={{0,8},{8,0},{16,24},{24,16},{1,9},{9,1},{17,25},{25,17},{2,10},{10... | collective-permute-start | bytes 3538952 | tf_op jit(solution)/shard_map/ppermute | solution.py:535
  14.6 58.8 %collective-permute-start.2 = (bf16[192,3072]{1,0:T(8,128)(2,1)}, bf16[192,3072]{1,0:T(8,128)(2,1)}, u32[]{:S(2)}, u32[]{:S(2)}) collective-permute-start(bf16[192,3072]{1,0:T(8,128)(2,1)} %get-tuple-element.243), channel_id=1, source_target_pairs={{0,16},{8,24},{16,0},{24,8},{1,17},{9,25},{17,1},{25,9},{2,18},{10... | collective-permute-start | bytes 3538952 | tf_op jit(solution)/shard_map/ppermute | solution.py:535
  45.9 31.7 %copy-start = (bf16[240,3072]{1,0:T(8,128)(2,1)}, bf16[240,3072]{1,0:T(8,128)(2,1)S(1)}, u32[]{:S(2)}) copy-start(bf16[240,3072]{1,0:T(8,128)(2,1)S(1)} %collective-permute-done.1.refs_4_) | copy-start | bytes 4423684
  48.0 31.2 %copy-start.1 = (bf16[240,3072]{1,0:T(8,128)(2,1)}, bf16[240,3072]{1,0:T(8,128)(2,1)S(1)}, u32[]{:S(2)}) copy-start(bf16[240,3072]{1,0:T(8,128)(2,1)S(1)} %collective-permute-done.3.refs_6_) | copy-start | bytes 4423684
  49.4 36.8 %collective-permute-start.5 = (bf16[240,3072]{1,0:T(8,128)(2,1)}, bf16[240,3072]{1,0:T(8,128)(2,1)}, u32[]{:S(2)}, u32[]{:S(2)}) collective-permute-start(bf16[240,3072]{1,0:T(8,128)(2,1)} %broadcast_select_fusion), channel_id=1, source_target_pairs={{8,0},{10,2},{12,4},{14,6},{0,8},{2,10},{4,12},{6,14},{24,16},{26,... | collective-permute-start | bytes 4423688 | tf_op jit(solution)/shard_map/ppermute | solution.py:545
  75.7 23.1 %collective-permute-start.4 = (bf16[192,3072]{1,0:T(8,128)(2,1)}, bf16[192,3072]{1,0:T(8,128)(2,1)}, u32[]{:S(2)}, u32[]{:S(2)}) collective-permute-start(bf16[192,3072]{1,0:T(8,128)(2,1)} %broadcast_select_fusion.1), channel_id=1, source_target_pairs={{8,0},{10,2},{12,4},{14,6},{0,8},{2,10},{4,12},{6,14},{24,16},{26,... | collective-permute-start | bytes 3538952 | tf_op jit(solution)/shard_map/ppermute | solution.py:545
  75.8 24.4 %collective-permute-start.6 = (bf16[192,3072]{1,0:T(8,128)(2,1)}, bf16[192,3072]{1,0:T(8,128)(2,1)}, u32[]{:S(2)}, u32[]{:S(2)}) collective-permute-start(bf16[192,3072]{1,0:T(8,128)(2,1)} %collective-permute-done.refs_3_), channel_id=1, source_target_pairs={{0,1},{1,0},{2,3},{3,2},{4,5},{5,4},{6,7},{7,6},{8,9},{9,8},{10,11... | collective-permute-start | bytes 3538952 | tf_op jit(solution)/shard_map/ppermute | solution.py:538
  76.9 2.2 collective-permute-start.12
  77.5 29.4 %collective-permute-start.7 = (bf16[240,3072]{1,0:T(8,128)(2,1)S(1)}, bf16[240,3072]{1,0:T(8,128)(2,1)}, u32[]{:S(2)}, u32[]{:S(2)}) collective-permute-start(bf16[240,3072]{1,0:T(8,128)(2,1)S(1)} %collective-permute-done.1.refs_4_), channel_id=1, source_target_pairs={{0,1},{1,0},{2,3},{3,2},{4,5},{5,4},{6,7},{7,6},{8,9},{9,8},{10,11... | collective-permute-start | bytes 4423688 | tf_op jit(solution)/shard_map/ppermute | solution.py:538
  79.2 0.8 copy-start.26
  79.2 27.8 %collective-permute-start.9 = (bf16[240,3072]{1,0:T(8,128)(2,1)S(1)}, bf16[240,3072]{1,0:T(8,128)(2,1)}, u32[]{:S(2)}, u32[]{:S(2)}) collective-permute-start(bf16[240,3072]{1,0:T(8,128)(2,1)S(1)} %collective-permute-done.3.refs_6_), channel_id=1, source_target_pairs={{0,1},{1,0},{2,3},{3,2},{4,5},{5,4},{6,7},{7,6},{8,9},{9,8},{10,11... | collective-permute-start | bytes 4423688 | tf_op jit(solution)/shard_map/ppermute | solution.py:538
  86.2 20.8 %collective-permute-start.11 = (bf16[240,3072]{1,0:T(8,128)(2,1)}, bf16[240,3072]{1,0:T(8,128)(2,1)}, u32[]{:S(2)}, u32[]{:S(2)}) collective-permute-start(bf16[240,3072]{1,0:T(8,128)(2,1)} %collective-permute-done.5.refs_8_), channel_id=1, source_target_pairs={{0,1},{1,0},{2,3},{3,2},{4,5},{5,4},{6,7},{7,6},{8,9},{9,8},{10,11... | collective-permute-start | bytes 4423688 | tf_op jit(solution)/shard_map/ppermute | solution.py:538
  98.8 7.6 %collective-permute-start.8 = (bf16[192,3072]{1,0:T(8,128)(2,1)}, bf16[192,3072]{1,0:T(8,128)(2,1)}, u32[]{:S(2)}, u32[]{:S(2)}) collective-permute-start(bf16[192,3072]{1,0:T(8,128)(2,1)} %collective-permute-done.2.refs_5_), channel_id=1, source_target_pairs={{0,1},{1,0},{2,3},{3,2},{4,5},{5,4},{6,7},{7,6},{8,9},{9,8},{10,11... | collective-permute-start | bytes 3538952 | tf_op jit(solution)/shard_map/ppermute | solution.py:538
  100.1 6.8 %collective-permute-start.10 = (bf16[192,3072]{1,0:T(8,128)(2,1)}, bf16[192,3072]{1,0:T(8,128)(2,1)}, u32[]{:S(2)}, u32[]{:S(2)}) collective-permute-start(bf16[192,3072]{1,0:T(8,128)(2,1)} %collective-permute-done.4.refs_7_), channel_id=1, source_target_pairs={{0,1},{1,0},{2,3},{3,2},{4,5},{5,4},{6,7},{7,6},{8,9},{9,8},{10,11... | collective-permute-start | bytes 3538952 | tf_op jit(solution)/shard_map/ppermute | solution.py:538
  100.9 5.5 %copy-start.28 = (s32[512]{0:T(512)}, s32[512]{0:T(512)S(1)}, u32[]{:S(2)}) copy-start(s32[512]{0:T(512)S(1)} %pad_add_fusion) | copy-start | bytes 6148
  101.8 2.9 copy-start.13
  101.8 3.0 copy-start.15
  101.8 3.7 %copy-start.27 = (bf16[256,768]{1,0:T(8,128)(2,1)S(1)}, bf16[256,768]{1,0:T(8,128)(2,1)}, u32[]{:S(2)}) copy-start(bf16[256,768]{1,0:T(8,128)(2,1)} %copy-done.26) | copy-start | bytes 1179652
  106.4 93.7 %collective-permute-start.13 = (bf16[256,768]{1,0:T(8,128)(2,1)S(1)}, bf16[256,768]{1,0:T(8,128)(2,1)S(1)}, u32[]{:S(2)}, u32[]{:S(2)}) collective-permute-start(bf16[256,768]{1,0:T(8,128)(2,1)S(1)} %get-tuple-element.245), channel_id=1, source_target_pairs={{0,1},{1,0},{2,3},{3,2},{4,5},{5,4},{6,7},{7,6},{8,9},{9,8},{10,11... | collective-permute-start | bytes 1179656 | tf_op jit(solution)/shard_map/ppermute | solution.py:538
  197.0 19.6 %collective-permute-start.14 = (bf16[256,768]{1,0:T(8,128)(2,1)}, bf16[256,768]{1,0:T(8,128)(2,1)S(1)}, u32[]{:S(2)}, u32[]{:S(2)}) collective-permute-start(bf16[256,768]{1,0:T(8,128)(2,1)} %get-tuple-element.160), channel_id=1, source_target_pairs={{0,24},{8,16},{16,8},{24,0},{1,25},{9,17},{17,9},{25,1},{2,26},{10... | collective-permute-start | bytes 1179656 | tf_op jit(solution)/shard_map/ppermute | solution.py:535
  198.6 18.1 %collective-permute-start.15 = (bf16[256,768]{1,0:T(8,128)(2,1)}, bf16[256,768]{1,0:T(8,128)(2,1)S(1)}, u32[]{:S(2)}, u32[]{:S(2)}) collective-permute-start(bf16[256,768]{1,0:T(8,128)(2,1)} %get-tuple-element.161), channel_id=1, source_target_pairs={{24,1},{26,3},{28,5},{30,7},{25,0},{27,2},{29,4},{31,6},{16,9},{18... | collective-permute-start | bytes 1179656 | tf_op jit(solution)/shard_map/ppermute | solution.py:545
  199.3 17.4 %collective-permute-start.16 = (bf16[256,768]{1,0:T(8,128)(2,1)}, bf16[256,768]{1,0:T(8,128)(2,1)S(1)}, u32[]{:S(2)}, u32[]{:S(2)}) collective-permute-start(bf16[256,768]{1,0:T(8,128)(2,1)} %get-tuple-element.162), channel_id=1, source_target_pairs={{0,1},{2,3},{4,5},{6,7},{1,0},{3,2},{5,4},{7,6},{8,9},{10,11},{12,... | collective-permute-start | bytes 1179656 | tf_op jit(solution)/shard_map/ppermute | solution.py:545
  201.0 15.7 %copy-start.8 = (bf16[256,768]{1,0:T(8,128)(2,1)S(1)}, bf16[256,768]{1,0:T(8,128)(2,1)}, u32[]{:S(2)}) copy-start(bf16[256,768]{1,0:T(8,128)(2,1)} %get-tuple-element.187) | copy-start | bytes 1179652
  201.0 17.1 %copy-start.9 = (bf16[256,768]{1,0:T(8,128)(2,1)S(1)}, bf16[256,768]{1,0:T(8,128)(2,1)}, u32[]{:S(2)}) copy-start(bf16[256,768]{1,0:T(8,128)(2,1)} %get-tuple-element.188) | copy-start | bytes 1179652
  201.0 17.9 %copy-start.10 = (bf16[256,768]{1,0:T(8,128)(2,1)S(1)}, bf16[256,768]{1,0:T(8,128)(2,1)}, u32[]{:S(2)}) copy-start(bf16[256,768]{1,0:T(8,128)(2,1)} %get-tuple-element.189) | copy-start | bytes 1179652
  201.0 19.4 %copy-start.11 = (bf16[256,768]{1,0:T(8,128)(2,1)S(1)}, bf16[256,768]{1,0:T(8,128)(2,1)}, u32[]{:S(2)}) copy-start(bf16[256,768]{1,0:T(8,128)(2,1)} %get-tuple-element.190) | copy-start | bytes 1179652
  216.6 24.0 %copy-start.16 = (bf16[256,768]{1,0:T(8,128)(2,1)}, bf16[256,768]{1,0:T(8,128)(2,1)S(1)}, u32[]{:S(2)}) copy-start(bf16[256,768]{1,0:T(8,128)(2,1)S(1)} %collective-permute-done.14.refs_7_) | copy-start | bytes 1179652
  216.7 23.9 %copy-start.17 = (bf16[256,768]{1,0:T(8,128)(2,1)}, bf16[256,768]{1,0:T(8,128)(2,1)S(1)}, u32[]{:S(2)}) copy-start(bf16[256,768]{1,0:T(8,128)(2,1)S(1)} %collective-permute-done.15.refs_8_) | copy-start | bytes 1179652
  216.7 23.9 %copy-start.18 = (bf16[256,768]{1,0:T(8,128)(2,1)}, bf16[256,768]{1,0:T(8,128)(2,1)S(1)}, u32[]{:S(2)}) copy-start(bf16[256,768]{1,0:T(8,128)(2,1)S(1)} %collective-permute-done.16.refs_2_) | copy-start | bytes 1179652
  216.7 23.9 %collective-permute-start.17 = (bf16[256,768]{1,0:T(8,128)(2,1)S(1)}, bf16[256,768]{1,0:T(8,128)(2,1)S(1)}, u32[]{:S(2)}, u32[]{:S(2)}) collective-permute-start(bf16[256,768]{1,0:T(8,128)(2,1)S(1)} %copy-done.8), channel_id=1, source_target_pairs={{0,8},{8,0},{16,24},{24,16},{1,9},{9,1},{17,25},{25,17},{2,10},{10... | collective-permute-start | bytes 1179656 | tf_op jit(solution)/shard_map/ppermute | solution.py:535
  218.1 22.5 %collective-permute-start.18 = (bf16[256,768]{1,0:T(8,128)(2,1)S(1)}, bf16[256,768]{1,0:T(8,128)(2,1)S(1)}, u32[]{:S(2)}, u32[]{:S(2)}) collective-permute-start(bf16[256,768]{1,0:T(8,128)(2,1)S(1)} %copy-done.9), channel_id=1, source_target_pairs={{8,1},{10,3},{12,5},{14,7},{9,0},{11,2},{13,4},{15,6},{0,9},{2,11}... | collective-permute-start | bytes 1179656 | tf_op jit(solution)/shard_map/ppermute | solution.py:545
  218.9 21.7 %collective-permute-start.19 = (bf16[256,768]{1,0:T(8,128)(2,1)S(1)}, bf16[256,768]{1,0:T(8,128)(2,1)S(1)}, u32[]{:S(2)}, u32[]{:S(2)}) collective-permute-start(bf16[256,768]{1,0:T(8,128)(2,1)S(1)} %copy-done.10), channel_id=1, source_target_pairs={{0,16},{8,24},{16,0},{24,8},{1,17},{9,25},{17,1},{25,9},{2,18},{10... | collective-permute-start | bytes 1179656 | tf_op jit(solution)/shard_map/ppermute | solution.py:535
  220.4 20.3 %collective-permute-start.20 = (bf16[256,768]{1,0:T(8,128)(2,1)S(1)}, bf16[256,768]{1,0:T(8,128)(2,1)S(1)}, u32[]{:S(2)}, u32[]{:S(2)}) collective-permute-start(bf16[256,768]{1,0:T(8,128)(2,1)S(1)} %copy-done.11), channel_id=1, source_target_pairs={{16,1},{18,3},{20,5},{22,7},{17,0},{19,2},{21,4},{23,6},{24,9},{26... | collective-permute-start | bytes 1179656 | tf_op jit(solution)/shard_map/ppermute | solution.py:545
  240.6 15.9 %copy-start.19 = (bf16[256,768]{1,0:T(8,128)(2,1)}, bf16[256,768]{1,0:T(8,128)(2,1)S(1)}, u32[]{:S(2)}) copy-start(bf16[256,768]{1,0:T(8,128)(2,1)S(1)} %collective-permute-done.17.refs_3_) | copy-start | bytes 1179652
  240.6 15.9 %copy-start.20 = (bf16[256,768]{1,0:T(8,128)(2,1)}, bf16[256,768]{1,0:T(8,128)(2,1)S(1)}, u32[]{:S(2)}) copy-start(bf16[256,768]{1,0:T(8,128)(2,1)S(1)} %collective-permute-done.18.refs_4_) | copy-start | bytes 1179652
  240.6 15.9 %copy-start.21 = (bf16[256,768]{1,0:T(8,128)(2,1)}, bf16[256,768]{1,0:T(8,128)(2,1)S(1)}, u32[]{:S(2)}) copy-start(bf16[256,768]{1,0:T(8,128)(2,1)S(1)} %collective-permute-done.19.refs_5_) | copy-start | bytes 1179652
  240.7 15.9 %copy-start.22 = (bf16[256,768]{1,0:T(8,128)(2,1)}, bf16[256,768]{1,0:T(8,128)(2,1)S(1)}, u32[]{:S(2)}) copy-start(bf16[256,768]{1,0:T(8,128)(2,1)S(1)} %collective-permute-done.20.refs_6_) | copy-start | bytes 1179652
  275.7 2.3 collective-permute-start.21
  277.9 4.4 %copy-start.23 = (bf16[256,768]{1,0:T(8,128)(2,1)}, bf16[256,768]{1,0:T(8,128)(2,1)S(1)}, u32[]{:S(2)}) copy-start(bf16[256,768]{1,0:T(8,128)(2,1)S(1)} %collective-permute-done.21.refs_2_) | copy-start | bytes 1179652
  279.1 1.9 collective-permute-start.28
  279.6 18.8 %copy-start.2 = (bf16[256,768]{1,0:T(8,128)(2,1)S(1)}, bf16[256,768]{1,0:T(8,128)(2,1)}, u32[]{:S(2)}) copy-start(bf16[256,768]{1,0:T(8,128)(2,1)} %get-tuple-element.235) | copy-start | bytes 1179652
  282.2 22.3 %copy-start.3 = (bf16[256,768]{1,0:T(8,128)(2,1)S(1)}, bf16[256,768]{1,0:T(8,128)(2,1)}, u32[]{:S(2)}) copy-start(bf16[256,768]{1,0:T(8,128)(2,1)} %get-tuple-element.236) | copy-start | bytes 1179652
  282.2 22.3 %copy-start.4 = (bf16[256,768]{1,0:T(8,128)(2,1)S(1)}, bf16[256,768]{1,0:T(8,128)(2,1)}, u32[]{:S(2)}) copy-start(bf16[256,768]{1,0:T(8,128)(2,1)} %get-tuple-element.237) | copy-start | bytes 1179652
  282.2 23.9 %copy-start.5 = (bf16[256,768]{1,0:T(8,128)(2,1)S(1)}, bf16[256,768]{1,0:T(8,128)(2,1)}, u32[]{:S(2)}) copy-start(bf16[256,768]{1,0:T(8,128)(2,1)} %get-tuple-element.238) | copy-start | bytes 1179652
  282.2 25.3 %copy-start.6 = (bf16[256,768]{1,0:T(8,128)(2,1)S(1)}, bf16[256,768]{1,0:T(8,128)(2,1)}, u32[]{:S(2)}) copy-start(bf16[256,768]{1,0:T(8,128)(2,1)} %get-tuple-element.239) | copy-start | bytes 1179652
  282.2 27.2 %copy-start.7 = (bf16[256,768]{1,0:T(8,128)(2,1)S(1)}, bf16[256,768]{1,0:T(8,128)(2,1)}, u32[]{:S(2)}) copy-start(bf16[256,768]{1,0:T(8,128)(2,1)} %get-tuple-element.240) | copy-start | bytes 1179652
  282.3 8.4 %collective-permute-start.29 = (bf16[2,80,768]{2,1,0:T(8,128)(2,1)S(1)}, bf16[2,80,768]{2,1,0:T(8,128)(2,1)}, u32[]{:S(2)}, u32[]{:S(2)}) collective-permute-start(bf16[2,80,768]{2,1,0:T(8,128)(2,1)S(1)} %constant_dynamic-slice_fusion.1), channel_id=1, source_target_pairs={{0,16},{8,24},{16,0},{24,8},{1,17},{9,25},{17,1},{25,9},{2,18},{10... | collective-permute-start | bytes 737288 | tf_op jit(solution)/shard_map/ppermute | solution.py:535
  291.7 4.9 %collective-permute-start.30 = (bf16[1,80,768]{2,1,0:T(8,128)(2,1)S(1)}, bf16[1,80,768]{2,1,0:T(8,128)(2,1)S(1)}, u32[]{:S(2)}, u32[]{:S(2)}) collective-permute-start(bf16[1,80,768]{2,1,0:T(8,128)(2,1)S(1)} %constant_dynamic-slice_fusion), channel_id=1, source_target_pairs={{0,8},{8,0},{16,24},{24,16},{1,9},{9,1},{17,25},{25,17},{2,10},{10... | collective-permute-start | bytes 368648 | tf_op jit(solution)/shard_map/ppermute | solution.py:535
  296.7 4.9 %collective-permute-start.31 = (bf16[80,768]{1,0:T(8,128)(2,1)S(1)}, bf16[80,768]{1,0:T(8,128)(2,1)S(1)}, u32[]{:S(2)}, u32[]{:S(2)}) collective-permute-start(bf16[80,768]{1,0:T(8,128)(2,1)S(1)} %fusion.1), channel_id=1, source_target_pairs={{0,2},{1,3},{2,0},{3,1},{4,6},{5,7},{6,4},{7,5},{8,10},{9,11},{10,... | collective-permute-start | bytes 368648 | tf_op jit(solution)/shard_map/ppermute | solution.py:538
  298.4 9.1 %collective-permute-start.22 = (bf16[256,768]{1,0:T(8,128)(2,1)S(1)}, bf16[256,768]{1,0:T(8,128)(2,1)S(1)}, u32[]{:S(2)}, u32[]{:S(2)}) collective-permute-start(bf16[256,768]{1,0:T(8,128)(2,1)S(1)} %copy-done.2), channel_id=1, source_target_pairs={{0,8},{8,0},{16,24},{24,16},{1,9},{9,1},{17,25},{25,17},{2,10},{10... | collective-permute-start | bytes 1179656 | tf_op jit(solution)/shard_map/ppermute | solution.py:535
  301.7 7.7 %collective-permute-start.32 = (bf16[80,768]{1,0:T(8,128)(2,1)S(1)}, bf16[80,768]{1,0:T(8,128)(2,1)S(1)}, u32[]{:S(2)}, u32[]{:S(2)}) collective-permute-start(bf16[80,768]{1,0:T(8,128)(2,1)S(1)} %add_convert_fusion.3), channel_id=1, source_target_pairs={{0,4},{1,5},{2,6},{3,7},{4,0},{5,1},{6,2},{7,3},{8,12},{9,13},{10,... | collective-permute-start | bytes 368648 | tf_op jit(solution)/shard_map/ppermute | solution.py:538
  304.5 11.5 %collective-permute-start.23 = (bf16[256,768]{1,0:T(8,128)(2,1)S(1)}, bf16[256,768]{1,0:T(8,128)(2,1)S(1)}, u32[]{:S(2)}, u32[]{:S(2)}) collective-permute-start(bf16[256,768]{1,0:T(8,128)(2,1)S(1)} %copy-done.3), channel_id=1, source_target_pairs={{8,1},{10,3},{12,5},{14,7},{9,0},{11,2},{13,4},{15,6},{0,9},{2,11}... | collective-permute-start | bytes 1179656 | tf_op jit(solution)/shard_map/ppermute | solution.py:545
  304.5 27.8 %collective-permute-start.24 = (bf16[256,768]{1,0:T(8,128)(2,1)S(1)}, bf16[256,768]{1,0:T(8,128)(2,1)}, u32[]{:S(2)}, u32[]{:S(2)}) collective-permute-start(bf16[256,768]{1,0:T(8,128)(2,1)S(1)} %copy-done.4), channel_id=1, source_target_pairs={{0,16},{8,24},{16,0},{24,8},{1,17},{9,25},{17,1},{25,9},{2,18},{10... | collective-permute-start | bytes 1179656 | tf_op jit(solution)/shard_map/ppermute | solution.py:535
  306.1 35.8 %collective-permute-start.25 = (bf16[256,768]{1,0:T(8,128)(2,1)S(1)}, bf16[256,768]{1,0:T(8,128)(2,1)}, u32[]{:S(2)}, u32[]{:S(2)}) collective-permute-start(bf16[256,768]{1,0:T(8,128)(2,1)S(1)} %copy-done.5), channel_id=1, source_target_pairs={{16,1},{18,3},{20,5},{22,7},{17,0},{19,2},{21,4},{23,6},{24,9},{26... | collective-permute-start | bytes 1179656 | tf_op jit(solution)/shard_map/ppermute | solution.py:545
  307.5 12.7 %copy-start.24 = (bf16[256,768]{1,0:T(8,128)(2,1)}, bf16[256,768]{1,0:T(8,128)(2,1)S(1)}, u32[]{:S(2)}) copy-start(bf16[256,768]{1,0:T(8,128)(2,1)S(1)} %collective-permute-done.22.refs_3_) | copy-start | bytes 1179652
  307.5 34.4 %collective-permute-start.26 = (bf16[256,768]{1,0:T(8,128)(2,1)S(1)}, bf16[256,768]{1,0:T(8,128)(2,1)}, u32[]{:S(2)}, u32[]{:S(2)}) collective-permute-start(bf16[256,768]{1,0:T(8,128)(2,1)S(1)} %copy-done.6), channel_id=1, source_target_pairs={{0,24},{8,16},{16,8},{24,0},{1,25},{9,17},{17,9},{25,1},{2,26},{10... | collective-permute-start | bytes 1179656 | tf_op jit(solution)/shard_map/ppermute | solution.py:535
  309.4 32.5 %collective-permute-start.27 = (bf16[256,768]{1,0:T(8,128)(2,1)S(1)}, bf16[256,768]{1,0:T(8,128)(2,1)}, u32[]{:S(2)}, u32[]{:S(2)}) collective-permute-start(bf16[256,768]{1,0:T(8,128)(2,1)S(1)} %copy-done.7), channel_id=1, source_target_pairs={{24,1},{26,3},{28,5},{30,7},{25,0},{27,2},{29,4},{31,6},{16,9},{18... | collective-permute-start | bytes 1179656 | tf_op jit(solution)/shard_map/ppermute | solution.py:545
  316.0 4.2 %copy-start.25 = (bf16[256,768]{1,0:T(8,128)(2,1)}, bf16[256,768]{1,0:T(8,128)(2,1)S(1)}, u32[]{:S(2)}) copy-start(bf16[256,768]{1,0:T(8,128)(2,1)S(1)} %collective-permute-done.23.refs_4_) | copy-start | bytes 1179652
  316.0 29.4 %collective-permute-start.33 = (bf16[80,768]{1,0:T(8,128)(2,1)S(1)}, bf16[80,768]{1,0:T(8,128)(2,1)S(1)}, u32[]{:S(2)}, u32[]{:S(2)}) collective-permute-start(bf16[80,768]{1,0:T(8,128)(2,1)S(1)} %add_convert_fusion.2), channel_id=1, source_target_pairs={{0,1},{1,0},{2,3},{3,2},{4,5},{5,4},{6,7},{7,6},{8,9},{9,8},{10,11... | collective-permute-start | bytes 368648 | tf_op jit(solution)/shard_map/ppermute | solution.py:538
